TPU v7x, 32 devices: a whole 2x2x4 slice. The times are simulated.
32 devices in a mesh: fsdp: 4 (over z), context: 2 (over core), tensor: 4 (over y, x).
Axes of the slice: x: 2, y: 2, z: 4, core: 2. Of those that a mesh axis runs over, the one named last changes fastest.
Arguments:
- tokens: bfloat16 [4, 1024, 1536], P('fsdp', 'context'), may hold values from -6 to 6
- segments: int32 [4, 1024], P('fsdp', 'context'), may hold values from 0 to 7, never falling along the last dimension, each value on 1 to 768 neighbouring positions
- cotangent: bfloat16 [4, 1024, 1536], P('fsdp', 'context'), may hold values from -6 to 6
- query_weight: bfloat16 [1536, 1536], P('fsdp', 'tensor'), may hold values from -0.15625 to 0.15625
- key_weight: bfloat16 [1536, 1536], P('fsdp', 'tensor'), may hold values from -0.15625 to 0.15625
- value_weight: bfloat16 [1536, 1536], P('fsdp', 'tensor'), may hold values from -0.15625 to 0.15625
- house_weight: bfloat16 [1536, 1536], P('fsdp', 'tensor'), may hold values from -0.15625 to 0.15625
- beta_weight: bfloat16 [1536, 12], P('fsdp', 'tensor'), may hold values from -0.15625 to 0.15625
- conv_weight: bfloat16 [12, 4, 128], P('tensor', None, 'fsdp'), may hold values from -3 to 3
- output_weight: bfloat16 [1536, 1536], P('tensor', 'fsdp'), may hold values from -0.625 to 0.625
- gate_weight: bfloat16 [1536, 4096], P('fsdp', 'tensor'), may hold values from -0.15625 to 0.15625
- up_weight: bfloat16 [1536, 4096], P('fsdp', 'tensor'), may hold values from -0.15625 to 0.15625
- down_weight: bfloat16 [4096, 1536], P('tensor', 'fsdp'), may hold values from -0.09375 to 0.09375
- first_gain: bfloat16 [1536], P('fsdp'), may hold values from 0.5 to 1.5
- second_gain: bfloat16 [1536], P('fsdp'), may hold values from 0.5 to 1.5
Outputs:
- result: bfloat16 [4, 1024, 1536], P('fsdp', 'context')
- grad_input: float32 [4, 1024, 1536], P('fsdp', 'context')
- grad_query: float32 [1536, 1536], P('fsdp', 'tensor')
- grad_key: float32 [1536, 1536], P('fsdp', 'tensor')
- grad_value: float32 [1536, 1536], P('fsdp', 'tensor')
- grad_house: float32 [1536, 1536], P('fsdp', 'tensor')
- grad_beta: float32 [1536, 12], P('fsdp', 'tensor')
- grad_conv: float32 [12, 4, 128], P('tensor', None, 'fsdp')
- grad_output: float32 [1536, 1536], P('tensor', 'fsdp')
- grad_gate: float32 [1536, 4096], P('fsdp', 'tensor')
- grad_up: float32 [1536, 4096], P('fsdp', 'tensor')
- grad_down: float32 [4096, 1536], P('tensor', 'fsdp')
- grad_first: float32 [1536], P('fsdp')
- grad_second: float32 [1536], P('fsdp')
Inputs may be any that keep to these rules, and one draw needn't show every extreme that they name: `segments`: within each sequence the document numbers never fall, every number from 0 to 7 occurs, each document has 1 to 768 tokens, and one document of each sequence has exactly 768.
All inputs are finite; a program needn't handle non-finite values.
Results may differ from a plain program's by a relative error of at most 0.02.
Values may be sent and summed in bfloat16 or wider, within the bound.
A program may use at most 192 MiB of HBM per device.

v0:
```python
import math

import jax
import jax.numpy as jnp
from jax import lax
from jax.sharding import PartitionSpec as P


def from_behind(value, axis, steps):
    count = lax.axis_size(axis)
    leading, last = (max(0, -steps), min(count, count - steps))
    return lax.ppermute(value, axis, [(source, source + steps) for source in range(leading, last)])


def product(former, latter):
    return jnp.dot(former, latter, precision=lax.Precision.HIGHEST)


def pair_low(former, latter):
    return jnp.dot(
        former.astype(jnp.bfloat16), latter.astype(jnp.bfloat16), preferred_element_type=jnp.float32
    )


def narrow(former, latter):
    return jnp.dot(former, latter, preferred_element_type=jnp.float32)


def back_dot(former, latter):
    return lax.dot_general(
        former, latter, (((1,), (1,)), ((), ())), preferred_element_type=jnp.float32
    )


def left_dot(former, latter):
    return lax.dot_general(
        former, latter, (((0,), (0,)), ((), ())), preferred_element_type=jnp.float32
    )


def rms_scale(values, gain_vec):
    return values * lax.rsqrt(jnp.mean(values * values, axis=-1, keepdims=True) + 1e-06) * gain_vec


def house_conv(values, prefix, kernel, doc_tags, prefix_tags):
    head_total, tap_count, head_width = kernel.shape
    tap_rows = jnp.transpose(kernel, (1, 0, 2)).reshape(tap_count, head_total * head_width)
    joined = jnp.concatenate([prefix, values], axis=values.ndim - 2)
    all_tags = jnp.concatenate([prefix_tags, doc_tags], axis=doc_tags.ndim - 1)
    length = values.shape[-2]
    running = jnp.zeros(values.shape, jnp.float32)
    for offset in range(tap_count):
        offset_at = tap_count - 1 - offset
        shifted = lax.slice_in_dim(joined, offset_at, offset_at + length, axis=joined.ndim - 2)
        shifted_tags = lax.slice_in_dim(
            all_tags, offset_at, offset_at + length, axis=all_tags.ndim - 1
        )
        same_doc = (shifted_tags == doc_tags)[..., None]
        running = running + jnp.where(same_doc, shifted, 0.0) * tap_rows[offset]
    activation = jax.nn.silu(running)
    per_head = activation.reshape(activation.shape[:-1] + (head_total, head_width))
    normed = per_head * lax.rsqrt(jnp.sum(per_head * per_head, axis=-1, keepdims=True) + 1e-06)
    return normed.reshape(activation.shape)


def triangle(house_rows, beta_rows, doc_tags, pair):
    length = house_rows.shape[0]
    places = jnp.arange(length)
    earlier = (places[:, None] > places[None, :]) & (doc_tags[:, None] == doc_tags[None, :])
    coupling = jnp.where(earlier, pair(house_rows, house_rows.T) * beta_rows[:, None], 0.0)
    return (jnp.eye(length, dtype=jnp.float32) + coupling, earlier)


def trans_keys(key_rows, house_rows, beta_rows, doc_tags, pair):
    system, earlier = triangle(house_rows, beta_rows, doc_tags, pair)
    right_side = jnp.where(earlier, pair(house_rows, key_rows.T) * beta_rows[:, None], 0.0)
    solved = jax.scipy.linalg.solve_triangular(system, right_side, lower=True)
    return key_rows - product(solved.T, house_rows)


def attend(queries, key_rows, house_rows, beta_rows, doc_tags, far_keys, far_tags, pair):
    system, earlier = triangle(house_rows, beta_rows, doc_tags, pair)
    length = queries.shape[0]
    places = jnp.arange(length)
    far_same = doc_tags[:, None] == far_tags[None, :]
    local_side = jnp.where(earlier, pair(house_rows, key_rows.T) * beta_rows[:, None], 0.0)
    far_side = jnp.where(far_same, pair(house_rows, far_keys.T) * beta_rows[:, None], 0.0)
    solved = jax.scipy.linalg.solve_triangular(
        system, jnp.concatenate([local_side, far_side], axis=1), lower=True
    )
    causal = places[:, None] >= places[None, :]
    reached = jnp.where(causal, pair(queries, house_rows.T), 0.0)
    raw_scores = pair(queries, jnp.concatenate([key_rows, far_keys], axis=0).T) - product(
        reached, solved
    )
    allowed = jnp.concatenate([causal & (doc_tags[:, None] == doc_tags[None, :]), far_same], axis=1)
    scores = jnp.where(allowed, raw_scores / math.sqrt(queries.shape[1]), -1e30)
    row_max = jnp.max(scores, axis=1, keepdims=True)
    powered = jnp.exp(scores - row_max)
    return powered / jnp.sum(powered, axis=1, keepdims=True)


def head_major(values, head_count):
    seq_count, length, total_width = values.shape
    shaped = values.reshape(seq_count, length, head_count, total_width // head_count)
    return jnp.transpose(shaped, (0, 2, 1, 3)).reshape(
        seq_count * head_count, length, total_width // head_count
    )


def token_major(values, seq_count):
    items, length, head_width = values.shape
    head_count = items // seq_count
    shaped = values.reshape(seq_count, head_count, length, head_width)
    return jnp.transpose(shaped, (0, 2, 1, 3)).reshape(seq_count, length, head_count * head_width)


def on_device(
    tokens,
    segments,
    cotangent,
    query_weight,
    key_weight,
    value_weight,
    house_weight,
    beta_weight,
    conv_weight,
    output_weight,
    gate_weight,
    up_weight,
    down_weight,
    first_gain,
    second_gain,
):
    seq_count, length, model_width = tokens.shape
    row_count = seq_count * length
    gathered = (
        lax.all_gather(query_weight, "fsdp", axis=0, tiled=True),
        lax.all_gather(key_weight, "fsdp", axis=0, tiled=True),
        lax.all_gather(value_weight, "fsdp", axis=0, tiled=True),
        lax.all_gather(house_weight, "fsdp", axis=0, tiled=True),
        lax.all_gather(beta_weight, "fsdp", axis=0, tiled=True),
        lax.all_gather(conv_weight, "fsdp", axis=2, tiled=True),
        lax.all_gather(output_weight, "fsdp", axis=1, tiled=True),
        lax.all_gather(gate_weight, "fsdp", axis=0, tiled=True),
        lax.all_gather(up_weight, "fsdp", axis=0, tiled=True),
        lax.all_gather(down_weight, "fsdp", axis=1, tiled=True),
        lax.all_gather(first_gain, "fsdp", axis=0, tiled=True),
        lax.all_gather(second_gain, "fsdp", axis=0, tiled=True),
    )
    (
        query_full,
        key_full,
        value_full,
        house_full,
        beta_full,
        conv_full,
        output_full,
        gate_full,
        up_full,
        down_full,
        gain_first,
        gain_second,
    ) = gathered
    head_count = beta_full.shape[1]
    tap_count = conv_full.shape[1]
    inner_width = query_full.shape[1]
    doc_tags = (segments + 1).astype(jnp.float32)
    item_tags = jnp.repeat(doc_tags, head_count, axis=0)
    stream = tokens.reshape(row_count, model_width).astype(jnp.float32)
    first_scale = gain_first.astype(jnp.float32)
    second_scale = gain_second.astype(jnp.float32)
    kernel = conv_full.astype(jnp.float32)
    normed = rms_scale(stream, first_scale).astype(jnp.bfloat16)
    queries = narrow(normed, query_full).astype(jnp.bfloat16)
    key_rows = narrow(normed, key_full).astype(jnp.bfloat16)
    value_rows = narrow(normed, value_full).astype(jnp.bfloat16)
    house_in = narrow(normed, house_full).astype(jnp.bfloat16)
    beta_raw = narrow(normed, beta_full)
    beta_all = 2.0 * jax.nn.sigmoid(beta_raw)
    shaped_in = house_in.reshape(seq_count, length, inner_width)
    rim_rows = shaped_in[:, length - tap_count + 1 :, :]
    rim_tags = doc_tags[:, length - tap_count + 1 :].astype(jnp.bfloat16)
    prefix_in, prefix_marks = from_behind((rim_rows, rim_tags), "context", 1)
    prefix_float = prefix_in.astype(jnp.float32)
    prefix_tags = prefix_marks.astype(jnp.float32)
    input_float = shaped_in.astype(jnp.float32)
    house_rows = house_conv(input_float, prefix_float, kernel, doc_tags, prefix_tags).astype(
        jnp.bfloat16
    )
    query_items = head_major(queries.reshape(seq_count, length, inner_width), head_count)
    key_items = head_major(key_rows.reshape(seq_count, length, inner_width), head_count)
    value_items = head_major(value_rows.reshape(seq_count, length, inner_width), head_count)
    house_items = head_major(house_rows, head_count)
    beta_items = jnp.transpose(beta_all.reshape(seq_count, length, head_count), (0, 2, 1)).reshape(
        seq_count * head_count, length
    )

    def send_keys(item_in):
        key_item, house_item, beta_item, tag_item = item_in
        return trans_keys(
            key_item.astype(jnp.float32),
            house_item.astype(jnp.float32),
            beta_item,
            tag_item,
            pair_low,
        ).astype(jnp.bfloat16)

    sent_keys = lax.map(send_keys, (key_items, house_items, beta_items, item_tags))
    remote_keys, remote_values, remote_marks = from_behind(
        (sent_keys, value_items, doc_tags.astype(jnp.bfloat16)), "context", 1
    )
    remote_tags = jnp.repeat(remote_marks.astype(jnp.float32), head_count, axis=0)

    def attend_item(item_in):
        (
            query_item,
            key_item,
            house_item,
            beta_item,
            tag_item,
            remote_key,
            remote_tag,
            value_item,
            remote_value,
        ) = item_in
        attn_probs = attend(
            query_item.astype(jnp.float32),
            key_item.astype(jnp.float32),
            house_item.astype(jnp.float32),
            beta_item,
            tag_item,
            remote_key.astype(jnp.float32),
            remote_tag,
            pair_low,
        ).astype(jnp.bfloat16)
        return narrow(attn_probs, jnp.concatenate([value_item, remote_value], axis=0))

    mixed_items = lax.map(
        attend_item,
        (
            query_items,
            key_items,
            house_items,
            beta_items,
            item_tags,
            remote_keys,
            remote_tags,
            value_items,
            remote_values,
        ),
    )
    mixed = token_major(mixed_items, seq_count).reshape(row_count, inner_width).astype(jnp.bfloat16)
    branch_out = lax.psum(narrow(mixed, output_full), "tensor")
    middle = stream + branch_out
    normed_two = rms_scale(middle, second_scale).astype(jnp.bfloat16)
    gate_value = narrow(normed_two, gate_full)
    up_value = narrow(normed_two, up_full)
    sigmoid_gate = jax.nn.sigmoid(gate_value)
    activation = gate_value * sigmoid_gate
    hidden = (activation * up_value).astype(jnp.bfloat16)
    ffn_out = lax.psum(narrow(hidden, down_full).astype(jnp.bfloat16), "tensor").astype(jnp.float32)
    result = (middle + ffn_out).astype(jnp.bfloat16).reshape(seq_count, length, model_width)
    grad_rows = cotangent.reshape(row_count, model_width)
    grad_stream = grad_rows.astype(jnp.float32)
    grad_hidden = back_dot(grad_rows, down_full)
    grad_down = left_dot(hidden, grad_rows)
    grad_gate_in = (
        grad_hidden * up_value * (sigmoid_gate + activation * (1.0 - sigmoid_gate))
    ).astype(jnp.bfloat16)
    grad_up_in = (grad_hidden * activation).astype(jnp.bfloat16)
    grad_gate = left_dot(normed_two, grad_gate_in)
    grad_up = left_dot(normed_two, grad_up_in)
    grad_normed_two = lax.psum(
        (back_dot(grad_gate_in, gate_full) + back_dot(grad_up_in, up_full)).astype(jnp.bfloat16),
        "tensor",
    ).astype(jnp.float32)
    unused_two, second_pull = jax.vjp(rms_scale, middle, second_scale)
    grad_middle_part, grad_second = second_pull(grad_normed_two)
    grad_middle = grad_stream + grad_middle_part
    grad_attn = grad_middle.astype(jnp.bfloat16)
    grad_output = left_dot(mixed, grad_attn)
    grad_mixed = back_dot(grad_attn, output_full).astype(jnp.bfloat16)
    grad_items = head_major(grad_mixed.reshape(seq_count, length, inner_width), head_count)

    def attend_back(item_in):
        (
            query_item,
            key_item,
            house_item,
            beta_item,
            tag_item,
            remote_key,
            remote_tag,
            value_item,
            remote_value,
            grad_item,
        ) = item_in

        def scored(query_arg, key_arg, house_arg, beta_arg, remote_arg):
            return attend(
                query_arg, key_arg, house_arg, beta_arg, tag_item, remote_arg, remote_tag, product
            )

        attn_probs, pullback = jax.vjp(
            scored,
            query_item.astype(jnp.float32),
            key_item.astype(jnp.float32),
            house_item.astype(jnp.float32),
            beta_item,
            remote_key.astype(jnp.float32),
        )
        low_probs = attn_probs.astype(jnp.bfloat16)
        both_values = jnp.concatenate([value_item, remote_value], axis=0)
        grad_probs = back_dot(grad_item, both_values)
        grad_both = left_dot(low_probs, grad_item)
        grad_query_item, grad_key_item, grad_house_item, grad_beta_item, grad_remote_key = pullback(
            grad_probs
        )
        item_length = query_item.shape[0]
        return (
            grad_query_item,
            grad_key_item,
            grad_house_item,
            grad_beta_item,
            grad_remote_key,
            grad_both[:item_length],
            grad_both[item_length:],
        )

    (
        query_grads,
        key_grads,
        house_grads,
        beta_grads,
        remote_key_grads,
        value_grads,
        remote_value_grads,
    ) = lax.map(
        attend_back,
        (
            query_items,
            key_items,
            house_items,
            beta_items,
            item_tags,
            remote_keys,
            remote_tags,
            value_items,
            remote_values,
            grad_items,
        ),
    )
    returned_keys, returned_values = from_behind(
        (remote_key_grads.astype(jnp.bfloat16), remote_value_grads.astype(jnp.bfloat16)),
        "context",
        -1,
    )

    def keys_back(item_in):
        key_item, house_item, beta_item, tag_item, grad_item = item_in

        def moved(key_arg, house_arg, beta_arg):
            return trans_keys(key_arg, house_arg, beta_arg, tag_item, product)

        unused_keys, pullback = jax.vjp(
            moved, key_item.astype(jnp.float32), house_item.astype(jnp.float32), beta_item
        )
        return pullback(grad_item.astype(jnp.float32))

    key_more, house_more, beta_more = lax.map(
        keys_back, (key_items, house_items, beta_items, item_tags, returned_keys)
    )
    grad_queries = (
        token_major(query_grads, seq_count).reshape(row_count, inner_width).astype(jnp.bfloat16)
    )
    grad_keys = (
        token_major(key_grads + key_more, seq_count)
        .reshape(row_count, inner_width)
        .astype(jnp.bfloat16)
    )
    grad_values = (
        token_major(value_grads + returned_values.astype(jnp.float32), seq_count)
        .reshape(row_count, inner_width)
        .astype(jnp.bfloat16)
    )
    grad_house_rows = token_major(house_grads + house_more, seq_count)
    beta_total = jnp.transpose(
        (beta_grads + beta_more).reshape(seq_count, head_count, length), (0, 2, 1)
    ).reshape(row_count, head_count)

    def conv_part(values_arg, prefix_arg, kernel_arg):
        return house_conv(values_arg, prefix_arg, kernel_arg, doc_tags, prefix_tags)

    unused_conv, conv_pull = jax.vjp(conv_part, input_float, prefix_float, kernel)
    grad_in_own, grad_prefix, grad_conv = conv_pull(grad_house_rows)
    returned_prefix = from_behind(grad_prefix.astype(jnp.bfloat16), "context", -1)
    padded_prefix = jnp.pad(
        returned_prefix.astype(jnp.float32), ((0, 0), (length - tap_count + 1, 0), (0, 0))
    )
    grad_house_in = (
        (grad_in_own + padded_prefix).reshape(row_count, inner_width).astype(jnp.bfloat16)
    )
    sigmoid_beta = jax.nn.sigmoid(beta_raw)
    grad_beta_raw = (beta_total * 2.0 * sigmoid_beta * (1.0 - sigmoid_beta)).astype(jnp.bfloat16)
    grad_normed = (
        back_dot(grad_queries, query_full)
        + back_dot(grad_keys, key_full)
        + back_dot(grad_values, value_full)
        + back_dot(grad_house_in, house_full)
        + back_dot(grad_beta_raw, beta_full)
    )
    grad_normed = lax.psum(grad_normed.astype(jnp.bfloat16), "tensor").astype(jnp.float32)
    unused_one, first_pull = jax.vjp(rms_scale, stream, first_scale)
    grad_stream_part, grad_first = first_pull(grad_normed)
    grad_input = (grad_middle + grad_stream_part).reshape(seq_count, length, model_width)
    grad_query = left_dot(normed, grad_queries)
    grad_key = left_dot(normed, grad_keys)
    grad_value = left_dot(normed, grad_values)
    grad_house = left_dot(normed, grad_house_in)
    grad_beta = left_dot(normed, grad_beta_raw)
    shares = (
        lax.psum_scatter(
            grad_query.astype(jnp.bfloat16), "fsdp", scatter_dimension=0, tiled=True
        ).astype(jnp.float32),
        lax.psum_scatter(
            grad_key.astype(jnp.bfloat16), "fsdp", scatter_dimension=0, tiled=True
        ).astype(jnp.float32),
        lax.psum_scatter(
            grad_value.astype(jnp.bfloat16), "fsdp", scatter_dimension=0, tiled=True
        ).astype(jnp.float32),
        lax.psum_scatter(
            grad_house.astype(jnp.bfloat16), "fsdp", scatter_dimension=0, tiled=True
        ).astype(jnp.float32),
        lax.psum_scatter(
            grad_beta.astype(jnp.bfloat16), "fsdp", scatter_dimension=0, tiled=True
        ).astype(jnp.float32),
        lax.psum_scatter(
            grad_conv.astype(jnp.bfloat16), "fsdp", scatter_dimension=2, tiled=True
        ).astype(jnp.float32),
        lax.psum_scatter(
            grad_output.astype(jnp.bfloat16), "fsdp", scatter_dimension=1, tiled=True
        ).astype(jnp.float32),
        lax.psum_scatter(
            grad_gate.astype(jnp.bfloat16), "fsdp", scatter_dimension=0, tiled=True
        ).astype(jnp.float32),
        lax.psum_scatter(
            grad_up.astype(jnp.bfloat16), "fsdp", scatter_dimension=0, tiled=True
        ).astype(jnp.float32),
        lax.psum_scatter(
            grad_down.astype(jnp.bfloat16), "fsdp", scatter_dimension=1, tiled=True
        ).astype(jnp.float32),
        lax.psum_scatter(
            grad_first.astype(jnp.bfloat16), "fsdp", scatter_dimension=0, tiled=True
        ).astype(jnp.float32),
        lax.psum_scatter(
            grad_second.astype(jnp.bfloat16), "fsdp", scatter_dimension=0, tiled=True
        ).astype(jnp.float32),
    )
    (
        share_query,
        share_key,
        share_value,
        share_house,
        share_beta,
        share_conv,
        share_output,
        share_gate,
        share_up,
        share_down,
        share_first,
        share_second,
    ) = shares
    totals = (
        lax.psum(share_query.astype(jnp.bfloat16), "context").astype(jnp.float32),
        lax.psum(share_key.astype(jnp.bfloat16), "context").astype(jnp.float32),
        lax.psum(share_value.astype(jnp.bfloat16), "context").astype(jnp.float32),
        lax.psum(share_house.astype(jnp.bfloat16), "context").astype(jnp.float32),
        lax.psum(share_beta.astype(jnp.bfloat16), "context").astype(jnp.float32),
        lax.psum(share_conv.astype(jnp.bfloat16), "context").astype(jnp.float32),
        lax.psum(share_output.astype(jnp.bfloat16), "context").astype(jnp.float32),
        lax.psum(share_gate.astype(jnp.bfloat16), "context").astype(jnp.float32),
        lax.psum(share_up.astype(jnp.bfloat16), "context").astype(jnp.float32),
        lax.psum(share_down.astype(jnp.bfloat16), "context").astype(jnp.float32),
        lax.psum(share_first.astype(jnp.bfloat16), "context").astype(jnp.float32),
        lax.psum(share_second.astype(jnp.bfloat16), "context").astype(jnp.float32),
    )
    return (
        result,
        grad_input,
        totals[0],
        totals[1],
        totals[2],
        totals[3],
        totals[4],
        totals[5],
        totals[6],
        totals[7],
        totals[8],
        totals[9],
        totals[10],
        totals[11],
    )


def solution(mesh):
    in_specs = (
        P("fsdp", "context", None),
        P("fsdp", "context"),
        P("fsdp", "context", None),
        P("fsdp", "tensor"),
        P("fsdp", "tensor"),
        P("fsdp", "tensor"),
        P("fsdp", "tensor"),
        P("fsdp", "tensor"),
        P("tensor", None, "fsdp"),
        P("tensor", "fsdp"),
        P("fsdp", "tensor"),
        P("fsdp", "tensor"),
        P("tensor", "fsdp"),
        P("fsdp"),
        P("fsdp"),
    )
    out_specs = (
        P("fsdp", "context", None),
        P("fsdp", "context", None),
        P("fsdp", "tensor"),
        P("fsdp", "tensor"),
        P("fsdp", "tensor"),
        P("fsdp", "tensor"),
        P("fsdp", "tensor"),
        P("tensor", None, "fsdp"),
        P("tensor", "fsdp"),
        P("fsdp", "tensor"),
        P("fsdp", "tensor"),
        P("tensor", "fsdp"),
        P("fsdp"),
        P("fsdp"),
    )
    return jax.shard_map(
        on_device, mesh=mesh, in_specs=in_specs, out_specs=out_specs, check_vma=False
    )
```

profile of v0, /device:TPU:0, one launch (start us, length us, event | category | flops | bytes accessed | tf_op | source)
XLA Modules:
  0.0 2036.9 jit_solution(8371395858346652339)
XLA Ops:
  17.7 13.4 all-gather
  31.2 14.7 all_gather.40
  46.9 13.3 all_gather.41
  77.9 28.9 %all-gather.17.cloned.1.call-done = bf16[1536,384]{1,0:T(8,128)(2,1)} async-done(((bf16[384,384]{1,0:T(8,128)(2,1)}), bf16[1536,384]{1,0:T(8,128)(2,1)}) %all-gather.17.cloned.1.call-update) | async-done | bytes 1179664 | tf_op jit(solution)/shard_map/all_gather | solution.py:140
  123.5 180.7 %while.76 = (s32[]{:T(128)}, bf16[3,512,128]{2,1,0:T(8,128)(2,1)}, bf16[3,512,128]{2,1,0:T(8,128)(2,1)}, f32[3,512]{1,0:T(4,128)}, bf16[3,512,128]{2,1,0:T(8,128...) while((s32[]{:T(128)}, bf16[3,512,128]{2,1,0:T(8,128)(2,1)}, ...), condition=%wide.region_3.5_spmd, body=%wide.region_2.4_spmd.sunk | while | flops 1549139968 | bytes 11034450 | solution.py:209
  135.1 40.8 %custom-call.39 = f32[4,128,128]{1,2,0:T(8,128)} custom-call(f32[4,128,128]{2,1,0:T(8,128)} %get-tuple-element.999), custom_call_target="InvertDiagBlocksLowerTriangular" | custom-call | tf_op jit(solution)/shard_map/while/body/eval_jaxpr/jit(_solve_triangular)/triangular_solve/custom-call.1 | solution.py:77
  195.4 40.8 %custom-call.39 = f32[4,128,128]{1,2,0:T(8,128)} custom-call(f32[4,128,128]{2,1,0:T(8,128)} %get-tuple-element.999), custom_call_target="InvertDiagBlocksLowerTriangular" | custom-call | tf_op jit(solution)/shard_map/while/body/eval_jaxpr/jit(_solve_triangular)/triangular_solve/custom-call.1 | solution.py:77
  255.6 40.8 %custom-call.39 = f32[4,128,128]{1,2,0:T(8,128)} custom-call(f32[4,128,128]{2,1,0:T(8,128)} %get-tuple-element.999), custom_call_target="InvertDiagBlocksLowerTriangular" | custom-call | tf_op jit(solution)/shard_map/while/body/eval_jaxpr/jit(_solve_triangular)/triangular_solve/custom-call.1 | solution.py:77
  310.2 212.6 %while.78 = (s32[]{:T(128)}, bf16[3,512,128]{1,2,0:T(8,128)(2,1)}, f32[3,512]{1,0:T(4,128)}, f32[3,512]{1,0:T(4,128)}, bf16[3,512,128]{2,1,0:T(8,128)(2,1)S(1)},...) while((s32[]{:T(128)}, bf16[3,512,128]{1,2,0:T(8,128)(2,1)}, ...), condition=%wide.region_7.10_spmd, body=%wide.region_4.9_spmd.sunk | while | flops 5787483136 | bytes 43566020 | solution.py:239
  324.3 40.8 %custom-call.41 = f32[4,128,128]{1,2,0:T(8,128)} custom-call(f32[4,128,128]{2,1,0:T(8,128)} %get-tuple-element.1016), custom_call_target="InvertDiagBlocksLowerTriangular" | custom-call | tf_op jit(solution)/shard_map/while/body/eval_jaxpr/jit(_solve_triangular)/triangular_solve/custom-call.0 | solution.py:88
  394.9 40.8 %custom-call.41 = f32[4,128,128]{1,2,0:T(8,128)} custom-call(f32[4,128,128]{2,1,0:T(8,128)} %get-tuple-element.1016), custom_call_target="InvertDiagBlocksLowerTriangular" | custom-call | tf_op jit(solution)/shard_map/while/body/eval_jaxpr/jit(_solve_triangular)/triangular_solve/custom-call.0 | solution.py:88
  465.6 40.8 %custom-call.41 = f32[4,128,128]{1,2,0:T(8,128)} custom-call(f32[4,128,128]{2,1,0:T(8,128)} %get-tuple-element.1016), custom_call_target="InvertDiagBlocksLowerTriangular" | custom-call | tf_op jit(solution)/shard_map/while/body/eval_jaxpr/jit(_solve_triangular)/triangular_solve/custom-call.0 | solution.py:88
  541.5 72.6 %all-reduce.20.cloned.1.call-done = f32[512,1536]{1,0:T(8,128)} async-done(((f32[512,1536]{1,0:T(8,128)}), f32[512,1536]{1,0:T(8,128)}) %all-reduce.20.cloned.1.call-update) | async-done | bytes 3145744 | tf_op jit(solution)/shard_map/psum | solution.py:254
  618.6 60.5 %all-gather.21.cloned.1.call-done = bf16[1536,1024]{1,0:T(8,128)(2,1)} async-done(((bf16[384,1024]{1,0:T(8,128)(2,1)}), bf16[1536,1024]{1,0:T(8,128)(2,1)}) %all-gather.21.cloned.1.call-update) | async-done | bytes 3145744 | tf_op jit(solution)/shard_map/all_gather | solution.py:145
  684.7 58.1 %all-gather.23.cloned.1.call-done = bf16[1536,1024]{1,0:T(8,128)(2,1)} async-done(((bf16[384,1024]{1,0:T(8,128)(2,1)}), bf16[1536,1024]{1,0:T(8,128)(2,1)}) %all-gather.23.cloned.1.call-update) | async-done | bytes 3145744 | tf_op jit(solution)/shard_map/all_gather | solution.py:146
  748.3 58.0 %all-gather.25.cloned.1.call-done = bf16[1024,1536]{1,0:T(8,128)(2,1)} async-done(((bf16[1024,384]{1,0:T(8,128)(2,1)}), bf16[1024,1536]{1,0:T(8,128)(2,1)}) %all-gather.25.cloned.1.call-update) | async-done | bytes 3145744 | tf_op jit(solution)/shard_map/all_gather | solution.py:147
  819.1 59.4 %all-reduce.22.cloned.1.call-done = bf16[512,1536]{1,0:T(8,128)(2,1)} async-done(((bf16[512,1536]{1,0:T(8,128)(2,1)}), bf16[512,1536]{1,0:T(8,128)(2,1)}) %all-reduce.22.cloned.1.call-update) | async-done | bytes 1572880 | tf_op jit(solution)/shard_map/psum | solution.py:274
  904.3 443.6 %while.80 = (s32[]{:T(128)}, bf16[3,512,128]{1,2,0:T(8,128)(2,1)}, f32[3,512,128]{1,2,0:T(8,128)}, f32[3,512,128]{1,2,0:T(8,128)}, f32[3,512]{1,0:T(4,128)}, /*i...) while((s32[]{:T(128)}, bf16[3,512,128]{1,2,0:T(8,128)(2,1)}, ...), condition=%wide.region_22.26_spmd, body=%wide.region_13.25_spmd.sunk | while | flops 23477551104 | bytes 228490512 | solution.py:339
  919.7 41.2 %custom-call.43 = f32[4,128,128]{1,2,0:T(8,128)} custom-call(f32[4,128,128]{2,1,0:T(8,128)} %get-tuple-element.1049), custom_call_target="InvertDiagBlocksLowerTriangular" | custom-call | tf_op jit(solution)/shard_map/while/body/eval_jaxpr/jvp(jit(_solve_triangular))/triangular_solve/custom-call.0 | solution.py:88
  1066.6 41.2 %custom-call.43 = f32[4,128,128]{1,2,0:T(8,128)} custom-call(f32[4,128,128]{2,1,0:T(8,128)} %get-tuple-element.1049), custom_call_target="InvertDiagBlocksLowerTriangular" | custom-call | tf_op jit(solution)/shard_map/while/body/eval_jaxpr/jvp(jit(_solve_triangular))/triangular_solve/custom-call.0 | solution.py:88
  1213.4 41.2 %custom-call.43 = f32[4,128,128]{1,2,0:T(8,128)} custom-call(f32[4,128,128]{2,1,0:T(8,128)} %get-tuple-element.1049), custom_call_target="InvertDiagBlocksLowerTriangular" | custom-call | tf_op jit(solution)/shard_map/while/body/eval_jaxpr/jvp(jit(_solve_triangular))/triangular_solve/custom-call.0 | solution.py:88
  1361.2 308.9 %while.82 = (s32[]{:T(128)}, f32[3,512,128]{1,2,0:T(8,128)}, f32[3,512,128]{1,2,0:T(8,128)}, f32[3,512]{1,0:T(4,128)}, bf16[3,512,128]{2,1,0:T(8,128)(2,1)}, /*i...) while((s32[]{:T(128)}, f32[3,512,128]{1,2,0:T(8,128)}, ...), condition=%wide.region_26.30_spmd, body=%wide.region_23.29_spmd.sunk | while | flops 7202799104 | bytes 67824904 | solution.py:371
  1389.8 39.3 %custom-call.45 = f32[4,128,128]{1,2,0:T(8,128)S(1)} custom-call(f32[4,128,128]{2,1,0:T(8,128)S(1)} %get-tuple-element.1078), custom_call_target="InvertDiagBlocksLowerTriangular" | custom-call | tf_op jit(solution)/shard_map/while/body/eval_jaxpr/transpose(jvp(jit(_solve_triangular)))/triangular_solve/custom-call.2 | solution.py:77
  1487.4 39.3 %custom-call.45 = f32[4,128,128]{1,2,0:T(8,128)S(1)} custom-call(f32[4,128,128]{2,1,0:T(8,128)S(1)} %get-tuple-element.1078), custom_call_target="InvertDiagBlocksLowerTriangular" | custom-call | tf_op jit(solution)/shard_map/while/body/eval_jaxpr/transpose(jvp(jit(_solve_triangular)))/triangular_solve/custom-call.2 | solution.py:77
  1584.9 39.3 %custom-call.45 = f32[4,128,128]{1,2,0:T(8,128)S(1)} custom-call(f32[4,128,128]{2,1,0:T(8,128)S(1)} %get-tuple-element.1078), custom_call_target="InvertDiagBlocksLowerTriangular" | custom-call | tf_op jit(solution)/shard_map/while/body/eval_jaxpr/transpose(jvp(jit(_solve_triangular)))/triangular_solve/custom-call.2 | solution.py:77
  1722.6 13.0 reduce-scatter.25.cloned.1.call-done
  1735.6 61.2 %reduce-scatter.27.cloned.1.call-done = bf16[384,1024]{1,0:T(8,128)(2,1)} async-done(((bf16[1536,1024]{1,0:T(8,128)(2,1)}), bf16[384,1024]{1,0:T(8,128)(2,1)}) %reduce-scatter.27.cloned.1.call-update) | async-done | bytes 786448 | tf_op jit(solution)/shard_map/reduce_scatter | solution.py:444
  1796.8 62.5 %reduce-scatter.29.cloned.1.call-done = bf16[384,1024]{1,0:T(8,128)(2,1)} async-done(((bf16[1536,1024]{1,0:T(8,128)(2,1)}), bf16[384,1024]{1,0:T(8,128)(2,1)}) %reduce-scatter.29.cloned.1.call-update) | async-done | bytes 786448 | tf_op jit(solution)/shard_map/reduce_scatter | solution.py:447
  1860.9 20.4 %reduce-scatter.33.cloned.1.call-done = bf16[32,12]{1,0:T(8,128)(2,1)} async-done(((bf16[128,12]{1,0:T(8,128)(2,1)}), bf16[32,12]{1,0:T(8,128)(2,1)}) %reduce-scatter.33.cloned.1.call-update) | async-done | bytes 784
  1882.1 20.8 %reduce-scatter.31.cloned.1.call-done = bf16[384,3]{1,0:T(8,128)(2,1)} async-done(((bf16[1536,3]{1,0:T(8,128)(2,1)}), bf16[384,3]{1,0:T(8,128)(2,1)}) %reduce-scatter.31.cloned.1.call-update) | async-done | bytes 2320
  1903.9 87.9 %all-reduce.24.cloned.1.call-done = (bf16[512,1536]{1,0:T(8,128)(2,1)}, bf16[512,1536]{1,0:T(8,128)(2,1)}) async-done(((bf16[512,1536]{1,0:T(8,128)(2,1)}, bf16[512,1536]{1,0:T(8,128)(2,1)}), (bf16[512,1536]{1,0:T(8,128)(2,1)}, bf16[512,1536]{1,0:T(8,128)(2,1)})) %all-reduce.24.cloned.1.call-update) | async-done | bytes 3145744 | tf_op jit(solution)/shard_map/psum | solution.py:262
  1995.0 11.9 all-reduce.12
  (1403 shorter events, 970.9 us)
Async XLA Ops:
  7.2 54.4 %all-gather.15.cloned.1.call-start = ((), (), s32[]{:S(2)}) async-start(), calls=%async_computation.12 | async-start | bytes 1474560 | tf_op jit(solution)/shard_map/all_gather | solution.py:141
  7.9 67.8 %all-gather.13.cloned.1.call-start = ((), (), s32[]{:S(2)}) async-start(), calls=%async_computation.11 | async-start | bytes 1474560 | tf_op jit(solution)/shard_map/all_gather | solution.py:139
  8.7 98.2 %all-gather.17.cloned.1.call-start = ((), (), s32[]{:S(2)}) async-start(), calls=%async_computation.13 | async-start | bytes 1474560 | tf_op jit(solution)/shard_map/all_gather | solution.py:140
  9.4 297.7 %all-gather.11.cloned.1.call-start = ((), (), s32[]{:S(2)}) async-start(), calls=%async_computation.10 | async-start | bytes 1474560 | tf_op jit(solution)/shard_map/all_gather | solution.py:138
  10.0 512.9 %all-gather.19.cloned.1.call-start = ((), (), s32[]{:S(2)}) async-start(), calls=%async_computation.14 | async-start | bytes 1474560 | tf_op jit(solution)/shard_map/all_gather | solution.py:144
  10.7 296.4 %collective-permute-start = (bf16[1,512]{1,0:T(2,128)(2,1)S(1)}, bf16[1,512]{1,0:T(2,128)(2,1)S(1)}, u32[]{:S(2)}, u32[]{:S(2)}) collective-permute-start(bf16[1,512]{1,0:T(2,128)(2,1)S(1)} %get-tuple-element.595), channel_id=1, source_target_pairs={{0,4},{1,5},{2,6},{3,7},{8,12},{9,13},{10,14},{11,15},{16,20},{17,... | collective-permute-start | bytes 3080 | tf_op jit(solution)/shard_map/ppermute | solution.py:12
  13.2 48.2 %collective-permute-start.1 = (bf16[1,3]{1,0:T(2,128)(2,1)S(1)}, bf16[1,3]{1,0:T(2,128)(2,1)S(1)}, u32[]{:S(2)}, u32[]{:S(2)}) collective-permute-start(bf16[1,3]{1,0:T(2,128)(2,1)S(1)} %slice.452), channel_id=1, source_target_pairs={{0,4},{1,5},{2,6},{3,7},{8,12},{9,13},{10,14},{11,15},{16,20},{17,... | collective-permute-start | bytes 26 | tf_op jit(solution)/shard_map/ppermute | solution.py:12
  14.5 599.6 %all-reduce.20.cloned.1.call-start = ((), (), s32[]{:S(2)}) async-start(), calls=%async_computation.15 | async-start | bytes 6291456 | tf_op jit(solution)/shard_map/psum | solution.py:254
  17.1 290.1 %copy-start.124 = (f32[512]{0:T(512)}, f32[512]{0:T(512)S(1)}, u32[]{:S(2)}) copy-start(f32[512]{0:T(512)S(1)} %fusion.451) | copy-start | bytes 6148
  31.1 276.1 %copy-start.104 = (f32[1536]{0:T(1024)}, f32[1536]{0:T(1024)S(1)}, u32[]{:S(2)}) copy-start(f32[1536]{0:T(1024)S(1)} %reshape.590) | copy-start | bytes 18436
  64.0 50.4 %collective-permute-start.2 = (bf16[1,3,384]{2,1,0:T(4,128)(2,1)S(1)}, bf16[1,3,384]{2,1,0:T(4,128)(2,1)S(1)}, u32[]{:S(2)}, u32[]{:S(2)}) collective-permute-start(bf16[1,3,384]{2,1,0:T(4,128)(2,1)S(1)} %slice.455), channel_id=1, source_target_pairs={{0,4},{1,5},{2,6},{3,7},{8,12},{9,13},{10,14},{11,15},{16,20},{17,... | collective-permute-start | bytes 6920 | tf_op jit(solution)/shard_map/ppermute | solution.py:12
  112.1 197.6 %collective-permute-start.4 = (bf16[3,512,128]{2,1,0:T(8,128)(2,1)S(1)}, bf16[3,512,128]{2,1,0:T(8,128)(2,1)}, u32[]{:S(2)}, u32[]{:S(2)}) collective-permute-start(bf16[3,512,128]{2,1,0:T(8,128)(2,1)S(1)} %bitcast.828), channel_id=1, source_target_pairs={{0,4},{1,5},{2,6},{3,7},{8,12},{9,13},{10,14},{11,15},{16,20},{17,... | collective-permute-start | bytes 1179656 | tf_op jit(solution)/shard_map/ppermute | solution.py:12
  304.2 5.4 collective-permute-start.3
  527.2 151.9 %all-gather.21.cloned.1.call-start = ((), (), s32[]{:S(2)}) async-start(), calls=%async_computation.16 | async-start | bytes 3932160 | tf_op jit(solution)/shard_map/all_gather | solution.py:145
  528.0 214.8 %all-gather.23.cloned.1.call-start = ((), (), s32[]{:S(2)}) async-start(), calls=%async_computation.17 | async-start | bytes 3932160 | tf_op jit(solution)/shard_map/all_gather | solution.py:146
  528.7 277.6 %all-gather.25.cloned.1.call-start = ((), (), s32[]{:S(2)}) async-start(), calls=%async_computation.18 | async-start | bytes 3932160 | tf_op jit(solution)/shard_map/all_gather | solution.py:147
  529.4 349.1 %all-reduce.22.cloned.1.call-start = ((), (), s32[]{:S(2)}) async-start(), calls=%async_computation.19 | async-start | bytes 3145728 | tf_op jit(solution)/shard_map/psum | solution.py:274
  819.1 899.3 %reduce-scatter.35.cloned.1.call-start = ((), (), s32[]{:S(2)}) async-start(), calls=%async_computation.28 | async-start | bytes 1474560
  886.6 833.7 %reduce-scatter.37.cloned.1.call-start = ((), (), s32[]{:S(2)}) async-start(), calls=%async_computation.29 | async-start | bytes 3932160
  894.1 828.5 %reduce-scatter.19.cloned.1.call-start = ((), (), s32[]{:S(2)}) async-start(), calls=%async_computation.20 | async-start | bytes 1474560 | tf_op jit(solution)/shard_map/reduce_scatter | solution.py:423
  1351.7 370.9 %reduce-scatter.23.cloned.1.call-start = ((), (), s32[]{:S(2)}) async-start(), calls=%async_computation.22 | async-start | bytes 1474560 | tf_op jit(solution)/shard_map/reduce_scatter | solution.py:429
  1351.7 3.7 collective-permute-start.6
  1353.2 5.5 collective-permute-start.5
  1358.6 364.0 %reduce-scatter.21.cloned.1.call-start = ((), (), s32[]{:S(2)}) async-start(), calls=%async_computation.21 | async-start | bytes 1474560 | tf_op jit(solution)/shard_map/reduce_scatter | solution.py:426
  1675.4 60.1 %reduce-scatter.25.cloned.1.call-start = ((), (), s32[]{:S(2)}) async-start(), calls=%async_computation.23 | async-start | bytes 1474560 | tf_op jit(solution)/shard_map/reduce_scatter | solution.py:432
  1682.9 3.2 collective-permute-start.7
  1688.4 108.4 %reduce-scatter.27.cloned.1.call-start = ((), (), s32[]{:S(2)}) async-start(), calls=%async_computation.24 | async-start | bytes 3932160 | tf_op jit(solution)/shard_map/reduce_scatter | solution.py:444
  1693.7 165.5 %reduce-scatter.29.cloned.1.call-start = ((), (), s32[]{:S(2)}) async-start(), calls=%async_computation.25 | async-start | bytes 3932160 | tf_op jit(solution)/shard_map/reduce_scatter | solution.py:447
  1699.0 182.3 %reduce-scatter.33.cloned.1.call-start = ((), (), s32[]{:S(2)}) async-start(), calls=%async_computation.27 | async-start | bytes 40960
  1708.8 194.2 %reduce-scatter.31.cloned.1.call-start = ((), (), s32[]{:S(2)}) async-start(), calls=%async_computation.26 | async-start | bytes 491520
  1710.4 281.5 %all-reduce.24.cloned.1.call-start = ((), (), s32[]{:S(2)}) async-start(), calls=%async_computation.30 | async-start | bytes 6291456 | tf_op jit(solution)/shard_map/psum | solution.py:262
  1718.4 302.1 %all-reduce.26.cloned.1.call-start = ((), (), s32[]{:S(2)}) async-start(), calls=%async_computation.31 | async-start | bytes 7667712 | tf_op jit(solution)/shard_map/psum | solution.py:475
  (276 other events, 2921.1 us)
Sparse Core Ops, SparseCore 0:
  9.6 34.8 all-gather.14
  46.1 29.6 all-gather.12
  77.3 29.4 all-gather.16
  108.3 29.6 all-gather.10
  139.4 28.9 all-gather.18
  527.3 86.6 all-reduce.19
  615.6 63.4 all-gather.20
  680.7 62.0 all-gather.22
  744.4 61.8 all-gather.24
  819.2 59.3 all-reduce.21
  886.7 29.3 reduce-scatter.34
  918.2 59.0 reduce-scatter.36
  1351.8 29.3 reduce-scatter.18
  1383.3 27.9 reduce-scatter.22
  1675.6 29.8 reduce-scatter.20
  1707.6 27.9 reduce-scatter.24
  1737.7 58.9 reduce-scatter.26
  1798.9 60.3 reduce-scatter.28
  1862.1 19.1 reduce-scatter.32
  1883.9 18.9 reduce-scatter.30
  1906.6 85.1 all-reduce.23
  1995.3 25.1 all-reduce.25
where the time goes:
time: 2050 us; the launch traced here: 2040 us
  waiting for transfers between devices  623 us (30%)
  other arithmetic  548 us (27%)
  matrix products  466 us (23%)
  local copies, waits for them, and re-layouts  274 us (13%)
  blocking collectives  67.7 us (3%)
  loops' own time  26.1 us (1%)
    another operation x21, other arithmetic, attend(): jax.scipy.linalg.solve_triangular(system, jnp.concatenate([local_side, fa...  246 us
    another operation x18, other arithmetic, trans_keys(): solved = jax.scipy.linalg.solve_triangular(system, right_side, lower=True)  240 us
    dot_general x84, matrix products, product(): return jnp.dot(former, latter, precision=lax.Precision.HIGHEST)  164 us
    psum x1, waiting for transfers between devices, on_device(): lax.psum(narrow(hidden, down_full).astype(jnp.bfloat16), 'tensor')  87.9 us
    another operation x84, matrix products, trans_keys(): solved = jax.scipy.linalg.solve_triangular(system, right_side, lower=True)  81.6 us
    another operation x84, matrix products, attend(): jax.scipy.linalg.solve_triangular(system, jnp.concatenate([local_side, fa...  78 us
    psum x1, waiting for transfers between devices, on_device(): branch_out = lax.psum(narrow(mixed, output_full), 'tensor')  72.6 us
    another operation x120, local copies, waits for them, and re-layouts, trans_keys(): solved = jax.scipy.linalg.solve_triangular(system, right_side, lower=True)  70.6 us
  transfers between devices with their start and end apart: 30, of which 16 were waited for; matrix products, arithmetic and copies ran while one was open for 61% of the time, Pallas kernels for 0%

commit v1 on v0

v1 whole, which is shorter than its diff:
```python
import functools
import math

import jax
import jax.numpy as jnp
from jax import lax
from jax.experimental import pallas as pl
from jax.experimental.pallas import tpu as pltpu
from jax.sharding import PartitionSpec as P

BF = jnp.bfloat16
F32 = jnp.float32
HALO = 16


def dot_nn(a, b):
    return jnp.dot(a, b, preferred_element_type=F32)


def dot_nt(a, b):
    return lax.dot_general(a, b, (((1,), (1,)), ((), ())), preferred_element_type=F32)


def dot_tn(a, b):
    return lax.dot_general(a, b, (((0,), (0,)), ((), ())), preferred_element_type=F32)


def iotas(rows, cols):
    return (
        lax.broadcasted_iota(jnp.int32, (rows, cols), 0),
        lax.broadcasted_iota(jnp.int32, (rows, cols), 1),
    )


def unit_lower_inverse(blocks, size):
    row, col = iotas(size, size)
    diff = row ^ col
    eye = jnp.where(row == col, 1.0, 0.0).astype(F32)
    low = row > col
    inv = [eye - jnp.where(low & (diff < 2), a, 0.0) for a in blocks]
    span = 2
    while span < size:
        pick = low & (diff >= span) & (diff < 2 * span)
        off = [jnp.where(pick, a, 0.0).astype(BF) for a in blocks]
        held = [t.astype(BF) for t in inv]
        step = [dot_nn(h, o).astype(BF) for h, o in zip(held, off)]
        inv = [t - dot_nn(s, h) for t, s, h in zip(inv, step, held)]
        span *= 2
    return inv


def conv_taps(hin, prefix, taps, marks):
    ext = jnp.concatenate([prefix, hin], axis=0)
    shifts = [hin]
    total = hin * taps[0:1, :]
    for lag in range(1, taps.shape[0]):
        moved = pltpu.roll(ext, lag, 0)[HALO:, :]
        moved = jnp.where(marks[:, lag : lag + 1] > 0.0, moved, 0.0)
        shifts.append(moved)
        total = total + moved * taps[lag : lag + 1, :]
    return total, shifts


def prep_kernel(k_ref, h_ref, pre_ref, tap_ref, mark_ref, b_ref, w_ref, t_ref, c_ref, sent_ref):
    length = k_ref.shape[0]
    half = length // 2
    quarter = length // 4
    heads = t_ref.shape[0]
    row, col = iotas(length, length)
    strict = row > col
    total, unused = conv_taps(
        h_ref[...].astype(F32), pre_ref[...].astype(F32), tap_ref[...], mark_ref[...]
    )
    act = total * jax.nn.sigmoid(total)
    houses, blocks, coupled = [], [], []
    for h in range(heads):
        cols = slice(h * 128, (h + 1) * 128)
        a = act[:, cols]
        w = (a * lax.rsqrt(jnp.sum(a * a, axis=1, keepdims=True) + 1e-06)).astype(BF)
        w_ref[:, cols] = w
        houses.append(w)
        full = jnp.where(strict, dot_nt(w, w) * b_ref[:, h * 128 : h * 128 + 1], 0.0)
        coupled.append(full.astype(BF))
        for q in range(4):
            blocks.append(full[q * quarter : (q + 1) * quarter, q * quarter : (q + 1) * quarter])
    inv = unit_lower_inverse(blocks, quarter)
    for h in range(heads):
        cols = slice(h * 128, (h + 1) * 128)
        diag = [t.astype(BF) for t in inv[4 * h : 4 * h + 4]]
        halves = []
        for p in range(2):
            at = p * half
            off = coupled[h][at + quarter : at + half, at : at + quarter]
            corner = -dot_nn(dot_nn(diag[2 * p + 1], off).astype(BF), diag[2 * p])
            zero = jnp.zeros((quarter, quarter), BF)
            halves.append(
                jnp.concatenate(
                    [
                        jnp.concatenate([diag[2 * p], zero], axis=1),
                        jnp.concatenate([corner.astype(BF), diag[2 * p + 1]], axis=1),
                    ],
                    axis=0,
                )
            )
        off = coupled[h][half:, :half]
        corner = -dot_nn(dot_nn(halves[1], off).astype(BF), halves[0])
        t_full = jnp.concatenate(
            [
                jnp.concatenate([halves[0], jnp.zeros((half, half), BF)], axis=1),
                jnp.concatenate([corner.astype(BF), halves[1]], axis=1),
            ],
            axis=0,
        )
        t_ref[h] = t_full
        w = houses[h]
        k = k_ref[:, cols]
        c = jnp.where(strict, dot_nt(w, k) * b_ref[:, h * 128 : h * 128 + 1], 0.0).astype(BF)
        c_ref[h] = c
        z = dot_tn(t_full, w).astype(BF)
        sent_ref[:, cols] = (k.astype(F32) - dot_tn(c, z)).astype(BF)


def attend_kernel(
    q_ref, k_ref, v_ref, w_ref, b_ref, t_ref, c_ref, fk_ref, fv_ref, tc_ref, tr_ref,
    o_ref, p_ref, x_ref, qt_ref,
):
    length = q_ref.shape[0]
    row, col = iotas(length, length)
    causal = row >= col
    q, k, w = q_ref[...], k_ref[...], w_ref[...]
    wb = (w.astype(F32) * b_ref[...]).astype(BF)
    reach = jnp.where(causal, dot_nt(q, w), 0.0).astype(BF)
    x = dot_nn(reach, t_ref[0]).astype(BF)
    x_ref[0] = x
    qt = (q.astype(F32) - dot_nn(x, wb)).astype(BF)
    qt_ref[...] = qt
    scale = 1.0 / math.sqrt(q.shape[1])
    tags = tc_ref[...]
    near = jnp.where(
        causal & (tags == tr_ref[0:1, :]), (dot_nt(q, k) - dot_nn(x, c_ref[0])) * scale, -1e30
    )
    far = jnp.where(tags == tr_ref[1:2, :], dot_nt(qt, fk_ref[...]) * scale, -1e30)
    top = jnp.maximum(
        jnp.max(near, axis=1, keepdims=True), jnp.max(far, axis=1, keepdims=True)
    )
    near = jnp.exp(near - top)
    far = jnp.exp(far - top)
    inv = 1.0 / (jnp.sum(near, axis=1, keepdims=True) + jnp.sum(far, axis=1, keepdims=True))
    near = (near * inv).astype(BF)
    far = (far * inv).astype(BF)
    p_ref[0, :, :length] = near
    p_ref[0, :, length:] = far
    o_ref[...] = (dot_nn(near, v_ref[...]) + dot_nn(far, fv_ref[...])).astype(BF)


def attend_back_kernel(
    g_ref, q_ref, k_ref, v_ref, w_ref, b_ref, t_ref, c_ref, fk_ref, fv_ref, p_ref, x_ref, qt_ref,
    dq_ref, dk_ref, dv_ref, dw_ref, dwb_ref, dfk_ref, dfv_ref,
):
    length = q_ref.shape[0]
    row, col = iotas(length, length)
    q, k, w, g = q_ref[...], k_ref[...], w_ref[...], g_ref[...]
    wb = (w.astype(F32) * b_ref[...]).astype(BF)
    x, t, c = x_ref[0], t_ref[0], c_ref[0]
    near, far = p_ref[0, :, :length], p_ref[0, :, length:]
    dv_ref[...] = dot_tn(near, g)
    dfv_ref[...] = dot_tn(far, g).astype(BF)
    d_near = dot_nt(g, v_ref[...])
    d_far = dot_nt(g, fv_ref[...])
    near, far = near.astype(F32), far.astype(F32)
    mean = jnp.sum(near * d_near, axis=1, keepdims=True) + jnp.sum(
        far * d_far, axis=1, keepdims=True
    )
    scale = 1.0 / math.sqrt(q.shape[1])
    s_near = (near * (d_near - mean) * scale).astype(BF)
    s_far = (far * (d_far - mean) * scale).astype(BF)
    dfk_ref[...] = dot_tn(s_far, qt_ref[...]).astype(BF)
    dqt = dot_nn(s_far, fk_ref[...])
    dqt_low = dqt.astype(BF)
    neg_dx = (dot_nt(s_near, c) + dot_nt(dqt_low, wb)).astype(BF)
    e = jnp.where(row >= col, -dot_nt(neg_dx, t), 0.0).astype(BF)
    dc = jnp.where(row > col, -dot_tn(x, s_near), 0.0).astype(BF)
    da = jnp.where(row > col, -dot_tn(x, e), 0.0).astype(BF)
    dq = dot_nn(
        jnp.concatenate([s_near, s_far, e], axis=1),
        jnp.concatenate([k, fk_ref[...], w], axis=0),
    )
    dq_ref[...] = dq.astype(BF)
    dk_ref[...] = dot_tn(s_near, q) + dot_tn(dc, wb)
    dwb_ref[...] = dot_nn(dc, k) - dot_tn(x, dqt_low) + dot_nn(da, w)
    dw_ref[...] = dot_tn(e, q) + dot_tn(da, wb)


def keys_back_kernel(
    d_ref, bv_ref, q_ref, k_ref, w_ref, b_ref, t_ref, c_ref, h_ref, pre_ref, tap_ref, mark_ref,
    dki_ref, dvi_ref, dwi_ref, dwbi_ref,
    out_ref, tail_ref, dpre_ref, dtap_ref,
):
    length, inner = k_ref.shape
    heads = inner // 128
    row, col = iotas(length, length)
    strict = row > col
    marks = mark_ref[...]
    lanes = lax.broadcasted_iota(jnp.int32, (length, 128), 1)
    side = jnp.zeros((length, 128), F32)
    out_ref[:, :inner] = q_ref[...]
    out_ref[:, 2 * inner : 3 * inner] = (dvi_ref[...] + bv_ref[...].astype(F32)).astype(BF)
    for h in range(heads):
        cols = slice(h * 128, (h + 1) * 128)
        k, w, d, b = k_ref[:, cols], w_ref[:, cols], d_ref[:, cols], b_ref[:, cols]
        wb = (w.astype(F32) * b).astype(BF)
        t, c = t_ref[h], c_ref[h]
        z = dot_tn(t, w).astype(BF)
        dc = jnp.where(strict, -dot_nt(z, d), 0.0).astype(BF)
        f = -dot_nn(t, dot_nn(c, d).astype(BF))
        da = jnp.where(strict, -dot_nt(z, f.astype(BF)), 0.0).astype(BF)
        dk = (dki_ref[:, cols] + d.astype(F32) + dot_tn(dc, wb)).astype(BF)
        out_ref[:, inner + h * 128 : inner + (h + 1) * 128] = dk
        dwb = dwbi_ref[:, cols] + dot_nn(dc, k) + dot_nn(da, w)
        dw = dwi_ref[:, cols] + f + dot_tn(da, wb) + b * dwb
        db = jnp.sum(dwb * w.astype(F32), axis=1, keepdims=True)
        side = jnp.where(lanes == h, db * (b * (1.0 - 0.5 * b)), side)
        taps = tap_ref[:, cols]
        total, shifts = conv_taps(
            h_ref[:, cols].astype(F32), pre_ref[:, cols].astype(F32), taps, marks
        )
        sig = jax.nn.sigmoid(total)
        act = total * sig
        r = lax.rsqrt(jnp.sum(act * act, axis=1, keepdims=True) + 1e-06)
        d_act = r * dw - act * (r * r * r * jnp.sum(act * dw, axis=1, keepdims=True))
        d_total = d_act * sig * (1.0 + total * (1.0 - sig))
        rows = [jnp.sum(d_total * s, axis=0, keepdims=True) for s in shifts]
        dtap_ref[:, cols] = jnp.concatenate(
            rows + [jnp.zeros((8 - len(rows), 128), F32)], axis=0
        )
        pad = jnp.zeros((HALO, 128), F32)
        out = jnp.concatenate([pad, d_total * taps[0:1, :]], axis=0)
        for lag in range(1, taps.shape[0]):
            part = jnp.where(marks[:, lag : lag + 1] > 0.0, d_total, 0.0) * taps[lag : lag + 1, :]
            out = out + pltpu.roll(jnp.concatenate([pad, part], axis=0), length + HALO - lag, 0)
        dpre_ref[:, cols] = out[:HALO, :].astype(BF)
        tail_ref[:, cols] = out[length:, :]
        out_ref[:, 3 * inner + h * 128 : 3 * inner + (h + 1) * 128] = out[HALO:, :].astype(BF)
    out_ref[:, 4 * inner :] = side.astype(BF)


def sds(shape, dtype):
    return jax.ShapeDtypeStruct(shape, dtype)


def cost(micros):
    return pl.CostEstimate(flops=micros * 10**9, bytes_accessed=micros * 10**6, transcendentals=0)


def params():
    return pltpu.CompilerParams(vmem_limit_bytes=56 * 1024 * 1024)


def call_prep(k, hin, prefix, taps, marks, beta):
    length, width = k.shape
    heads = width // 128
    whole = pl.BlockSpec(memory_space=pltpu.VMEM)
    return pl.pallas_call(
        prep_kernel,
        out_shape=(
            sds((length, width), BF),
            sds((heads, length, length), BF),
            sds((heads, length, length), BF),
            sds((length, width), BF),
        ),
        in_specs=[whole] * 6,
        out_specs=[whole] * 4,
        compiler_params=params(),
        cost_estimate=cost(9),
        name="prep",
    )(k, hin, prefix, taps, marks, beta)


def head_specs(length):
    slab = pl.BlockSpec((length, 128), lambda h: (0, h))
    square = pl.BlockSpec((1, length, length), lambda h: (h, 0, 0))
    double = pl.BlockSpec((1, length, 2 * length), lambda h: (h, 0, 0))
    return slab, square, double


def fixed(shape):
    return pl.BlockSpec(shape, lambda h: (0,) * len(shape))


def call_attend(q, k, v, w, beta, t, c, fk, fv, tag_col, tag_rows):
    length, width = q.shape
    heads = width // 128
    slab, square, double = head_specs(length)
    return pl.pallas_call(
        attend_kernel,
        grid=(heads,),
        out_shape=(
            sds((length, width), BF),
            sds((heads, length, 2 * length), BF),
            sds((heads, length, length), BF),
            sds((length, width), BF),
        ),
        in_specs=[slab] * 5
        + [square, square, slab, slab, fixed(tag_col.shape), fixed(tag_rows.shape)],
        out_specs=[slab, double, square, slab],
        compiler_params=params(),
        cost_estimate=cost(11),
        name="attend",
    )(q, k, v, w, beta, t, c, fk, fv, tag_col, tag_rows)


def call_attend_back(g, q, k, v, w, beta, t, c, fk, fv, p, x, qt):
    length, width = q.shape
    heads = width // 128
    slab, square, double = head_specs(length)
    flat = (length, width)
    return pl.pallas_call(
        attend_back_kernel,
        grid=(heads,),
        out_shape=(
            sds(flat, BF), sds(flat, F32), sds(flat, F32), sds(flat, F32), sds(flat, F32),
            sds(flat, BF), sds(flat, BF),
        ),
        in_specs=[slab] * 6 + [square, square, slab, slab, double, square, slab],
        out_specs=[slab] * 7,
        compiler_params=params(),
        cost_estimate=cost(16),
        name="attend_back",
    )(g, q, k, v, w, beta, t, c, fk, fv, p, x, qt)


def call_keys_back(d, back_v, dq, k, w, beta, t, c, hin, prefix, taps, marks, dk, dv, dw, dwb):
    length, width = k.shape
    whole = pl.BlockSpec(memory_space=pltpu.VMEM)
    return pl.pallas_call(
        keys_back_kernel,
        out_shape=(
            sds((length, 4 * width + 128), BF), sds((HALO, width), F32), sds((HALO, width), BF),
            sds((8, width), F32),
        ),
        in_specs=[whole] * 16,
        out_specs=[whole] * 4,
        compiler_params=params(),
        cost_estimate=cost(10),
        name="keys_back",
    )(d, back_v, dq, k, w, beta, t, c, hin, prefix, taps, marks, dk, dv, dw, dwb)


def exchange(mesh_size, name, ident, lhs, rhs, transposed, extras, finish, rows_out, wide_type):
    length = lhs.shape[0]
    model = rhs.shape[0] if transposed else rhs.shape[1]
    n = mesh_size
    chunk = length // n
    many = len(extras)

    def body(*refs):
        lhs_ref, rhs_ref = refs[:2]
        extra_refs = refs[2 : 2 + many]
        out_ref, *row_refs = refs[2 + many : 3 + many + len(rows_out)]
        send, recv, held, send_a, recv_a, send_b, recv_b = refs[3 + many + len(rows_out) :]
        me = lax.axis_index("tensor")
        barrier = pltpu.get_barrier_semaphore()
        peers = [lax.rem(me + i, n) for i in range(1, n)]
        for peer in peers:
            pl.semaphore_signal(
                barrier, inc=1, device_id={"tensor": peer}, device_id_type=pl.DeviceIdType.MESH
            )
        pl.semaphore_wait(barrier, n - 1)

        def rows_of(index):
            return pl.ds(pl.multiple_of(index * chunk, chunk), chunk)

        def partial(index):
            left = lhs_ref[rows_of(index), :]
            return dot_nt(left, rhs_ref[...]) if transposed else dot_nn(left, rhs_ref[...])

        first = []
        for i, peer in enumerate(peers):
            send[i] = partial(peer).astype(BF)
            copy = pltpu.make_async_remote_copy(
                src_ref=send.at[i], dst_ref=recv.at[i],
                send_sem=send_a.at[i], recv_sem=recv_a.at[i],
                device_id={"tensor": peer}, device_id_type=pl.DeviceIdType.MESH,
            )
            copy.start()
            first.append(copy)
        total = partial(me)
        for i, copy in enumerate(first):
            copy.wait()
            total = total + recv[i].astype(F32)
        mine = rows_of(me)
        done, *row_values = finish(total, mine, *extra_refs)
        held[mine, :] = done.astype(BF)
        second = []
        for i, peer in enumerate(peers):
            copy = pltpu.make_async_remote_copy(
                src_ref=held.at[mine, :], dst_ref=held.at[mine, :],
                send_sem=send_b.at[i], recv_sem=recv_b.at[i],
                device_id={"tensor": peer}, device_id_type=pl.DeviceIdType.MESH,
            )
            copy.start()
            second.append(copy)
        for ref, value in zip(row_refs, row_values):
            ref[...] = value
        for copy in second:
            copy.wait()
        out_ref[...] = held[...].astype(wide_type)

    whole = pl.BlockSpec(memory_space=pltpu.VMEM)
    return pl.pallas_call(
        body,
        out_shape=(sds((length, model), wide_type),)
        + tuple(sds((chunk if r is None else r, model), F32) for r in rows_out),
        in_specs=[whole] * (2 + many),
        out_specs=[whole] * (1 + len(rows_out)),
        scratch_shapes=[
            pltpu.VMEM((n - 1, chunk, model), BF),
            pltpu.VMEM((n - 1, chunk, model), BF),
            pltpu.VMEM((length, model), BF),
            pltpu.SemaphoreType.DMA((n - 1,)),
            pltpu.SemaphoreType.DMA((n - 1,)),
            pltpu.SemaphoreType.DMA((n - 1,)),
            pltpu.SemaphoreType.DMA((n - 1,)),
        ],
        compiler_params=pltpu.CompilerParams(
            vmem_limit_bytes=56 * 1024 * 1024, collective_id=ident, has_side_effects=True
        ),
        cost_estimate=cost(40),
        name=name,
    )(lhs, rhs, *extras)


def inverse_rms(x):
    return lax.rsqrt(jnp.mean(x * x, axis=1, keepdims=True) + 1e-06)


def finish_middle(total, mine, tokens_ref, gain_ref):
    middle = tokens_ref[mine, :].astype(F32) + total
    return middle * inverse_rms(middle) * gain_ref[0:1, :], middle


def finish_result(total, mine, middle_ref):
    return (middle_ref[...] + total,)


def norm_back(grad, x, gain):
    r = inverse_rms(x)
    g = grad * gain
    out = r * g - x * (r * r * r * jnp.mean(g * x, axis=1, keepdims=True))
    gain_grad = jnp.sum(grad * x * r, axis=0, keepdims=True)
    return out, jnp.broadcast_to(gain_grad, (8, gain_grad.shape[1]))


def finish_second(total, mine, middle_ref, cot_ref, gain_ref):
    out, gain_grad = norm_back(total, middle_ref[...], gain_ref[0:1, :])
    grad = cot_ref[mine, :].astype(F32) + out
    return grad, grad, gain_grad


def finish_first(total, mine, tokens_ref, grad_ref, gain_ref):
    out, gain_grad = norm_back(total, tokens_ref[mine, :].astype(F32), gain_ref[0:1, :])
    return grad_ref[...] + out, gain_grad


def shift_to(value, axis, steps):
    count = lax.axis_size(axis)
    leading, last = (max(0, -steps), min(count, count - steps))
    return lax.ppermute(value, axis, [(at, at + steps) for at in range(leading, last)])


def own_half(value):
    rows = value.shape[0] // lax.axis_size("context")
    return lax.dynamic_slice_in_dim(value, lax.axis_index("context") * rows, rows, axis=0)


def gather_rows(value):
    return lax.all_gather(own_half(value), ("fsdp", "context"), axis=0, tiled=True)


def gather_cols(value):
    rows, cols = value.shape
    deep, cores = lax.axis_size("fsdp"), lax.axis_size("context")
    parts = lax.all_gather(own_half(value), ("fsdp", "context"), axis=0, tiled=True)
    parts = parts.reshape(deep, rows, cols)
    return jnp.transpose(parts, (1, 0, 2)).reshape(rows, deep * cols)


def scatter_rows(value):
    part = lax.psum_scatter(value, ("fsdp", "context"), scatter_dimension=0, tiled=True)
    return lax.all_gather(part, "context", axis=0, tiled=True)


def scatter_cols(value):
    rows, cols = value.shape
    deep = lax.axis_size("fsdp")
    parts = jnp.transpose(value.reshape(rows, deep, cols // deep), (1, 0, 2))
    return scatter_rows(parts.reshape(deep * rows, cols // deep))


def on_device(
    tokens,
    segments,
    cotangent,
    query_weight,
    key_weight,
    value_weight,
    house_weight,
    beta_weight,
    conv_weight,
    output_weight,
    gate_weight,
    up_weight,
    down_weight,
    first_gain,
    second_gain,
):
    seq_count, length, model = tokens.shape
    rows = first_gain.shape[0]
    deep = lax.axis_size("fsdp")
    inner = query_weight.shape[1]
    heads, tap_count, chans = conv_weight.shape
    assert seq_count == 1 and heads * tap_count * chans == rows
    side = jnp.concatenate(
        [
            beta_weight,
            first_gain[:, None],
            second_gain[:, None],
            conv_weight.reshape(rows, 1),
            jnp.zeros((rows, 128 - heads - 3), BF),
        ],
        axis=1,
    )
    pack = gather_rows(
        jnp.concatenate([query_weight, key_weight, value_weight, house_weight, side], axis=1)
    )
    out_down = gather_cols(jnp.concatenate([output_weight, down_weight], axis=0))
    gate_up = gather_rows(jnp.concatenate([gate_weight, up_weight], axis=1))
    output_full, down_full = out_down[:inner], out_down[inner:]
    side_full = pack[:, 4 * inner :]
    gain_one = side_full[:, heads].astype(F32)
    gain_two = side_full[:, heads + 1].astype(F32)
    taps = jnp.transpose(
        side_full[:, heads + 2].reshape(deep, heads, tap_count, chans), (2, 1, 0, 3)
    ).reshape(tap_count, inner).astype(F32)

    tags = (segments[0] + 1).astype(F32)
    far_tags = shift_to(tags, "context", 1)
    near_tags = jnp.concatenate([far_tags[length - tap_count + 1 :], tags])
    marks = jnp.stack(
        [
            near_tags[tap_count - 1 - lag : tap_count - 1 - lag + length] == tags
            for lag in range(tap_count)
        ],
        axis=1,
    ).astype(F32)

    stream = tokens[0].astype(F32)
    scale_one = lax.rsqrt(jnp.mean(stream * stream, axis=1, keepdims=True) + 1e-06)
    normed = (stream * scale_one * gain_one).astype(BF)
    proj = dot_nn(normed, pack[:, : 4 * inner]).astype(BF)
    beta_raw = dot_nn(normed, side_full)[:, :heads]
    beta = jnp.repeat(2.0 * jax.nn.sigmoid(beta_raw), 128, axis=1)
    q, k, v, hin = (proj[:, i * inner : (i + 1) * inner] for i in range(4))
    prefix = shift_to(hin[length - HALO :], "context", 1)
    w, t, c, sent = call_prep(k, hin, prefix, taps, marks, beta)
    far_k = shift_to(sent, "context", 1)
    far_v = shift_to(v, "context", 1)
    mixed, probs, x, qt = call_attend(
        q, k, v, w, beta, t, c, far_k, far_v, tags[:, None], jnp.stack([tags, far_tags])
    )
    n = lax.axis_size("tensor")
    rows_one = jnp.broadcast_to(gain_one[None, :], (8, model))
    rows_two = jnp.broadcast_to(gain_two[None, :], (8, model))
    normed_two, middle = exchange(
        n, "sum_mixed", 1, mixed, output_full, False, (tokens[0], rows_two), finish_middle,
        (None,), BF,
    )

    both = dot_nn(normed_two, gate_up)
    hidden_width = both.shape[1] // 2
    gate, up = both[:, :hidden_width], both[:, hidden_width:]
    sig = jax.nn.sigmoid(gate)
    act = gate * sig
    hidden = (act * up).astype(BF)
    grad_rows = cotangent[0]
    grad_hidden = dot_nt(grad_rows, down_full)
    grad_both = jnp.concatenate(
        [grad_hidden * up * (sig + act * (1.0 - sig)), grad_hidden * act], axis=1
    ).astype(BF)
    grad_down = scatter_cols(dot_tn(hidden, grad_rows).astype(BF))
    grad_gate_up = scatter_rows(dot_tn(normed_two, grad_both).astype(BF))
    grad_attn, grad_middle, grad_second = exchange(
        n, "sum_second", 2, grad_both, gate_up, True, (middle, grad_rows, rows_two),
        finish_second, (None, 8), BF,
    )
    grad_output = scatter_cols(dot_tn(mixed, grad_attn).astype(BF))
    grad_mixed = dot_nt(grad_attn, output_full).astype(BF)

    dq, dk, dv, dw, dwb, dfk, dfv = call_attend_back(
        grad_mixed, q, k, v, w, beta, t, c, far_k, far_v, probs, x, qt
    )
    back_k = shift_to(dfk, "context", -1)
    back_v = shift_to(dfv, "context", -1)
    dproj, tail, dpre, dtap = call_keys_back(
        back_k, back_v, dq, k, w, beta, t, c, hin, prefix, taps, marks, dk, dv, dw, dwb
    )
    back_pre = shift_to(dpre, "context", -1).astype(F32)
    dproj = lax.dynamic_update_slice(
        dproj, (tail + back_pre).astype(BF), (length - HALO, 3 * inner)
    )
    grad_input, grad_first = exchange(
        n, "sum_first", 3, dproj, pack, True, (tokens[0], grad_middle, rows_one),
        finish_first, (8,), F32,
    )
    (result,) = exchange(
        n, "sum_hidden", 4, hidden, down_full, False, (middle,), finish_result, (), BF
    )
    grad_pack = dot_tn(normed, dproj).astype(BF)
    dconv = jnp.transpose(
        dtap[:tap_count].reshape(tap_count, heads, deep, chans), (2, 1, 0, 3)
    ).reshape(model, 1)
    side_cols = lax.broadcasted_iota(jnp.int32, (model, 128), 1)
    side_back = jnp.where(
        side_cols == heads + 2, dconv.astype(BF), grad_pack[:, 4 * inner :]
    )
    shares = scatter_rows(
        jnp.concatenate([grad_pack[:, : 4 * inner], side_back], axis=1)
    ).astype(F32)
    gains = lax.psum(
        jnp.stack([grad_first[0], grad_second[0]]), ("fsdp", "context", "tensor")
    )
    gains = lax.dynamic_slice_in_dim(gains, lax.axis_index("fsdp") * rows, rows, axis=1)
    grad_gate_up = grad_gate_up.astype(F32)
    return (
        result.reshape(tokens.shape),
        grad_input.reshape(tokens.shape),
        shares[:, :inner],
        shares[:, inner : 2 * inner],
        shares[:, 2 * inner : 3 * inner],
        shares[:, 3 * inner : 4 * inner],
        shares[:, 4 * inner : 4 * inner + heads],
        shares[:, 4 * inner + heads + 2].reshape(conv_weight.shape),
        grad_output.astype(F32),
        grad_gate_up[:, :hidden_width],
        grad_gate_up[:, hidden_width:],
        grad_down.astype(F32),
        gains[0],
        gains[1],
    )


def solution(mesh):
    in_specs = (
        P("fsdp", "context", None),
        P("fsdp", "context"),
        P("fsdp", "context", None),
        P("fsdp", "tensor"),
        P("fsdp", "tensor"),
        P("fsdp", "tensor"),
        P("fsdp", "tensor"),
        P("fsdp", "tensor"),
        P("tensor", None, "fsdp"),
        P("tensor", "fsdp"),
        P("fsdp", "tensor"),
        P("fsdp", "tensor"),
        P("tensor", "fsdp"),
        P("fsdp"),
        P("fsdp"),
    )
    out_specs = (
        P("fsdp", "context", None),
        P("fsdp", "context", None),
        P("fsdp", "tensor"),
        P("fsdp", "tensor"),
        P("fsdp", "tensor"),
        P("fsdp", "tensor"),
        P("fsdp", "tensor"),
        P("tensor", None, "fsdp"),
        P("tensor", "fsdp"),
        P("fsdp", "tensor"),
        P("fsdp", "tensor"),
        P("tensor", "fsdp"),
        P("fsdp"),
        P("fsdp"),
    )
    return jax.shard_map(
        on_device, mesh=mesh, in_specs=in_specs, out_specs=out_specs, check_vma=False
    )
```

time: 2050 us -> 555 us (0.27)
  other arithmetic: 548 us -> 16.7 us
  waiting for transfers between devices: 623 us -> 134 us
  matrix products: 466 us -> 38.8 us
  Pallas kernels: 0 us -> 224 us
  local copies, waits for them, and re-layouts: 274 us -> 57 us
  loops' own time: 26.1 us -> 0 us
    another operation x42 -> x3, other arithmetic: 487 us -> 0.63 us  [the longest x1 0.6 us: on_device(): jnp.stack([tags, far_tags])]
    dot_general x147 -> x9, matrix products: 306 us -> 38.8 us  [the longest x4 19 us: dot_tn(): lax.dot_general(a, b, (((0,), (0,)), ((), ())), preferred_element_type=F32)]
    pallas_call x0 -> x8, Pallas kernels: none -> 224 us  [the longest x4 176 us: exchange(): pl.pallas_call(body, out_shape=(sds((length, model), wide_type),) + tuple...]
    psum x4 -> x0, waiting for transfers between devices: 222 us -> none  [the longest x1 87.9 us: on_device(): lax.psum(narrow(hidden, down_full).astype(jnp.bfloat16), 'tensor')]
    another operation x168 -> x0, matrix products: 160 us -> none  [the longest x84 81.6 us: trans_keys(): solved = jax.scipy.linalg.solve_triangular(system, right_side, lower=True)]
    all_gather x8 -> x5, waiting for transfers between devices: 216 us -> 69.5 us  [the longest x2 50 us: gather_rows(): lax.all_gather(own_half(value), ('fsdp', 'context'), axis=0, tiled=True)]
    another operation x210 -> x5, local copies, waits for them, and re-layouts: 144 us -> 0.9 us  [the longest x1 0.69 us: on_device(): shares[:, 4 * inner + heads + 2].reshape(conv_weight.shape)]
    reduce_scatter x6 -> x4, waiting for transfers between devices: 137 us -> 60 us  [scatter_rows(): lax.psum_scatter(value, ('fsdp', 'context'), scatter_dimension=0, tiled=T...]
  transfers between devices with their start and end apart: 30 -> 16, of which waited for: 16 -> 8; matrix products, arithmetic and copies ran while one was open for 61% -> 13% of each run, Pallas kernels for 0% -> 27%
where the time goes in v1:
time: 555 us; the launch traced here: 546 us
  Pallas kernels  224 us (40%)
  waiting for transfers between devices  134 us (24%)
  local copies, waits for them, and re-layouts  57 us (10%)
  blocking collectives  48.2 us (9%)
  matrix products  38.8 us (7%)
  other arithmetic  16.7 us (3%)
  between operations  14.8 us (3%)
  starting transfers between devices  13.4 us (2%)
    pallas_call x4, Pallas kernels, exchange(): pl.pallas_call(body, out_shape=(sds((length, model), wide_type),) + tuple...  176 us
    reduce_scatter x4, waiting for transfers between devices, scatter_rows(): lax.psum_scatter(value, ('fsdp', 'context'), scatter_dimension=0, tiled=T...  60 us
    all_gather x2, waiting for transfers between devices, gather_rows(): lax.all_gather(own_half(value), ('fsdp', 'context'), axis=0, tiled=True)  50 us
    psum x1, blocking collectives, on_device(): lax.psum(jnp.stack([grad_first[0], grad_second[0]]), ('fsdp', 'context',...  43.4 us
    all_gather x1, waiting for transfers between devices, gather_cols(): lax.all_gather(own_half(value), ('fsdp', 'context'), axis=0, tiled=True)  19.5 us
    dot_general x4, matrix products, dot_tn(): lax.dot_general(a, b, (((0,), (0,)), ((), ())), preferred_element_type=F32)  19 us
    pallas_call x1, Pallas kernels, call_attend_back(): pl.pallas_call(attend_back_kernel, grid=(heads,), out_shape=(sds(flat, BF...  16.5 us
    reshape x1, local copies, waits for them, and re-layouts, gather_cols(): parts = parts.reshape(deep, rows, cols)  13.2 us
  transfers between devices with their start and end apart: 16, of which 8 were waited for; matrix products, arithmetic and copies ran while one was open for 13% of the time, Pallas kernels for 27%

profile of v1, /device:TPU:0, one launch (start us, length us, event | category | flops | bytes accessed | tf_op | source)
XLA Modules:
  0.0 546.4 jit_solution(2045138059075765341)
XLA Ops:
  10.6 2.4 concatenate.19
  17.3 2.5 collective-permute-start.1
  21.8 50.0 %all-gather.6.cloned.1.call-done.refs_1_ = bf16[1536,1664]{1,0:T(8,128)(2,1)} async-done(((bf16[192,1664]{1,0:T(8,128)(2,1)}), bf16[1536,1664]{1,0:T(8,128)(2,1)}) %all-gather.6.cloned.1.call-update) | async-done | bytes 5111824 | tf_op jit(solution)/shard_map/all_gather | solution.py:477
  71.8 2.2 convert_reduce_fusion.1
  74.0 5.0 fusion.5
  79.0 2.1 collective-permute-start
  88.5 9.0 %prep.1 = (bf16[512,384]{1,0:T(8,128)(2,1)}, bf16[3,512,512]{2,1,0:T(8,128)(2,1)}, bf16[3,512,512]{2,1,0:T(8,128)(2,1)}, bf16[512,384]{1,0:T(8,128)(2,1)}) custom-call(bf16[512,384]{1,0:T(8,128)(2,1)} %get-tuple-element.120.k_ref, bf16[512,384]{1,0:T(8,128)(2,1)} %get-tuple-element.118.h_ref, bf16[16,384]{1,0:T(8,128)(2,1)} %copy-done.24, ...), custom_call_target="tpu_custom_call" | custom-call | flops 8999999488 | bytes 9000000 | tf_op jit(solution)/shard_map/prep/pallas_call | solution.py:263
  97.5 2.2 collective-permute-start.2
  101.2 19.5 %all-gather.8.cloned.1.call-done = bf16[5632,384]{1,0:T(8,128)(2,1)} async-done(((bf16[704,384]{1,0:T(8,128)(2,1)}), bf16[5632,384]{1,0:T(8,128)(2,1)}) %all-gather.8.cloned.1.call-update) | async-done | bytes 4325392 | tf_op jit(solution)/shard_map/all_gather | solution.py:483
  120.7 13.2 %copy.80 = bf16[4,1408,384]{2,0,1:T(4,128)(2,1)S(1)} copy(bf16[4,1408,384]{2,1,0:T(8,128)(2,1)} %bitcast.64) | data formatting | bytes 8650752 | tf_op jit(solution)/shard_map/reshape | solution.py:484
  137.4 10.4 %attend.1 = (bf16[512,384]{1,0:T(8,128)(2,1)}, bf16[3,512,1024]{2,1,0:T(8,128)(2,1)}, bf16[3,512,512]{2,1,0:T(8,128)(2,1)}, bf16[512,384]{1,0:T(8,128)(2,1)}) custom-call(bf16[512,384]{1,0:T(8,128)(2,1)} %get-tuple-element.121.q_ref, bf16[512,384]{1,0:T(8,128)(2,1)} %get-tuple-element.120.k_ref, bf16[512,384]{1,0:T(8,128)(2,1)} %copy-done.13, ...), custom_call_target="tpu_custom_call" | custom-call | flops 11000000512 | bytes 11000000 | tf_op jit(solution)/shard_map/attend/pallas_call | solution.py:294
  148.4 44.1 %sum_mixed.1 = (bf16[512,1536]{1,0:T(8,128)(2,1)}, f32[128,1536]{1,0:T(8,128)}) custom-call(bf16[512,384]{1,0:T(8,128)(2,1)} %get-tuple-element.44.refs_0_, bf16[384,1536]{1,0:T(8,128)(2,1)} %bitcast.72, bf16[512,1536]{1,0:T(8,128)(2,1)} %bitcast.69, f32[8,1536]{1,0:T(8,128)} %broadcast_in_dim.39.refs_3_.refs_4_), custom_call_target="tpu_custom_call" | custom-call | flops 40000000000 | bytes 40000000 | tf_op jit(solution)/shard_map/sum_mixed/pallas_call | solution.py:410
  192.5 6.5 %fusion.29 = f32[512,2048]{1,0:T(8,128)S(1)} fusion(bf16[512,1536]{1,0:T(8,128)(2,1)} %get-tuple-element.45, bf16[1536,2048]{1,0:T(8,128)(2,1)} %all-gather.10.cloned.1.call-done.refs_1_), kind=kOutput, calls=%fused_computation.66 | convolution fusion | flops 3221225472 | bytes 12058624 | tf_op jit(solution)/shard_map/dot_general | solution.py:17
  199.1 3.5 fusion.9
  204.6 48.3 %sum_second.1 = (bf16[512,1536]{1,0:T(8,128)(2,1)}, f32[128,1536]{1,0:T(8,128)}, f32[8,1536]{1,0:T(8,128)}) custom-call(bf16[512,2048]{1,0:T(8,128)(2,1)} %pad_maximum_fusion.1.refs_0_, bf16[1536,2048]{1,0:T(8,128)(2,1)} %all-gather.10.cloned.1.call-done.refs_1_, f32[128,1536]{1,0:T(8,128)} %get-tuple-element.46.refs_2_, bf16[512,1536]{1,0:T(8,128)(2,1)} %bitcast.80, ...), custom_call_target="tpu_custom_call" | custom-call | flops 40000000000 | bytes 40000000 | tf_op jit(solution)/shard_map/sum_second/pallas_call | solution.py:410
  252.9 3.2 convolution_convert_fusion.4.g_ref
  256.0 16.5 %attend_back.1 = (bf16[512,384]{1,0:T(8,128)(2,1)}, f32[512,384]{1,0:T(8,128)}, f32[512,384]{1,0:T(8,128)}, f32[512,384]{1,0:T(8,128)}, f32[512,384]{1,0:T(8,128...) custom-call(bf16[512,384]{1,0:T(8,128)(2,1)} %convolution_convert_fusion.4.g_ref, ...), custom_call_target="tpu_custom_call" | custom-call | flops 16000000000 | bytes 16000000 | tf_op jit(solution)/shard_map/attend_back/pallas_call | solution.py:317
  278.4 11.6 %keys_back.1 = (bf16[512,1664]{1,0:T(8,128)(2,1)}, f32[16,384]{1,0:T(8,128)}, bf16[16,384]{1,0:T(8,128)(2,1)}, f32[8,384]{1,0:T(8,128)}) custom-call(bf16[512,384]{1,0:T(8,128)(2,1)} %copy-done.22, bf16[512,384]{1,0:T(8,128)(2,1)} %copy-done.23, bf16[512,384]{1,0:T(8,128)(2,1)} %get-tuple-element.53.q_ref, bf16[512,384]{1,0:T(8,128)(2,1)} %get-tuple-element.120.k_ref, ...), custom_call_target="tpu_custom_call" | custom-call | flops 10000000000 | bytes 10000000 | tf_op jit(solution)/shard_map/keys_back/pallas_call | solution.py:335
  294.7 5.2 convolution_convert_fusion
  300.5 2.6 pad_maximum_fusion
  304.7 6.9 %convolution_convert_fusion.1 = bf16[1536,2048]{1,0:T(8,128)(2,1)} fusion(bf16[512,1536]{1,0:T(8,128)(2,1)} %get-tuple-element.45, bf16[512,1024]{1,0:T(8,128)(2,1)S(1)} %copy-done.10, bf16[512,1024]{1,0:T(8,128)(2,1)S(1)} %copy-done.8), kind=kOutput, calls=%fused_computation.1 | convolution fusion | flops 3228565504 | bytes 9961472 | tf_op jit(solution)/shard_map/dot_general | solution.py:25
  312.6 2.2 convolution_convert_fusion.3
  316.9 4.7 convolution_convert_fusion.2
  321.7 5.0 reshape.129
  328.8 31.1 %reduce-scatter.5.cloned.1.call-done = bf16[192,1664]{1,0:T(8,128)(2,1)} async-done(((bf16[1536,1664]{1,0:T(8,128)(2,1)}), bf16[192,1664]{1,0:T(8,128)(2,1)}) %reduce-scatter.5.cloned.1.call-update) | async-done | bytes 638992 | tf_op jit(solution)/shard_map/reduce_scatter | solution.py:489
  360.3 40.3 %sum_hidden.1 = bf16[512,1536]{1,0:T(8,128)(2,1)} custom-call(bf16[512,1024]{1,0:T(8,128)(2,1)} %get-tuple-element.115.refs_0_, bf16[1024,1536]{1,0:T(8,128)(2,1)} %bitcast.66, f32[128,1536]{1,0:T(8,128)} %get-tuple-element.46.refs_2_), custom_call_target="tpu_custom_call" | custom-call | flops 40000000000 | bytes 40000000 | tf_op jit(solution)/shard_map/sum_hidden/pallas_call | solution.py:410
  401.4 28.9 %reduce-scatter.9.cloned.1.call-done = bf16[192,2048]{1,0:T(8,128)(2,1)} async-done(((bf16[1536,2048]{1,0:T(8,128)(2,1)}), bf16[192,2048]{1,0:T(8,128)(2,1)}) %reduce-scatter.9.cloned.1.call-update) | async-done | bytes 786448 | tf_op jit(solution)/shard_map/reduce_scatter | solution.py:489
  431.0 43.5 %sum_first.1 = (f32[512,1536]{1,0:T(8,128)}, f32[8,1536]{1,0:T(8,128)}) custom-call(bf16[512,1664]{1,0:T(8,128)(2,1)} %fusion.18.refs_0_, bf16[1536,1664]{1,0:T(8,128)(2,1)} %all-gather.6.cloned.1.call-done.refs_1_, bf16[512,1536]{1,0:T(8,128)(2,1)} %bitcast.70, f32[128,1536]{1,0:T(8,128)} %get-tuple-element.61.refs_3_, f32[8,1536]{1,0:T(8,128)} %broadcast_in_dim.40.refs_4_), custom_call_target="tpu_custom_call" | custom-call | flops 40000000000 | bytes 40000000 | tf_op jit(solution)/shard_map/sum_first/pallas_call | solution.py:410
  475.3 43.4 %psum.7 = f32[2,1536]{1,0:T(2,128)S(1)} all-reduce(f32[2,1536]{1,0:T(2,128)S(1)} %pad_maximum_fusion.2), channel_id=1, replica_groups=mesh['fsdp'=4,'context'=2,'tensor'=4] {'fsdp','context','tensor'}, use_global_device_ids=true, to_apply=%region_5.6 | all-reduce | flops 3072 | bytes 24576 | tf_op jit(solution)/shard_map/psum | solution.py:629
  519.4 2.2 all_gather.25
  522.5 2.6 all_gather.27
  531.7 3.5 fusion.26
  (149 shorter events, 57.1 us)
Async XLA Ops:
  7.2 64.6 %all-gather.6.cloned.1.call-start = ((), (), s32[]{:S(2)}) async-start(), calls=%async_computation.4 | async-start | bytes 5750784 | tf_op jit(solution)/shard_map/all_gather | solution.py:477
  10.6 3.4 copy-start.14
  13.0 3.1 copy-start.11
  13.1 3.1 copy-start.12
  14.0 106.8 %all-gather.8.cloned.1.call-start = ((), (), s32[]{:S(2)}) async-start(), calls=%async_computation.5 | async-start | bytes 4866048 | tf_op jit(solution)/shard_map/all_gather | solution.py:483
  16.1 3.7 copy-start.3
  16.1 176.4 %all-gather.10.cloned.1.call-start = ((), (), s32[]{:S(2)}) async-start(), calls=%async_computation.6 | async-start | bytes 7077888 | tf_op jit(solution)/shard_map/all_gather | solution.py:477
  17.2 342.7 %reduce-scatter.5.cloned.1.call-start = ((), (), s32[]{:S(2)}) async-start(), calls=%async_computation.7 | async-start | bytes 5750784 | tf_op jit(solution)/shard_map/reduce_scatter | solution.py:489
  17.3 3.3 collective-permute-start.1
  20.2 61.0 %copy-start.18 = (f32[512]{0:T(512)}, f32[512]{0:T(512)S(1)}, u32[]{:S(2)}) copy-start(f32[512]{0:T(512)S(1)} %add_rsqrt_fusion) | copy-start | bytes 6148
  74.0 7.2 %copy-start.15 = (f32[1536]{0:T(1024)}, f32[1536]{0:T(1024)S(1)}, u32[]{:S(2)}) copy-start(f32[1536]{0:T(1024)S(1)} %get-tuple-element.110) | copy-start | bytes 18436
  79.0 8.9 %collective-permute-start = (bf16[16,384]{1,0:T(8,128)(2,1)S(1)}, bf16[16,384]{1,0:T(8,128)(2,1)S(1)}, u32[]{:S(2)}, u32[]{:S(2)}) collective-permute-start(bf16[16,384]{1,0:T(8,128)(2,1)S(1)} %slice.158), channel_id=1, source_target_pairs={{0,4},{1,5},{2,6},{3,7},{8,12},{9,13},{10,14},{11,15},{16,20},{17,... | collective-permute-start | bytes 36872 | tf_op jit(solution)/shard_map/ppermute | solution.py:468
  83.9 13.7 %copy-start.13 = (bf16[512,384]{1,0:T(8,128)(2,1)}, bf16[512,384]{1,0:T(8,128)(2,1)S(1)}, u32[]{:S(2)}) copy-start(bf16[512,384]{1,0:T(8,128)(2,1)S(1)} %get-tuple-element.119.v_ref) | copy-start | bytes 1179652
  85.9 51.5 %collective-permute-start.3 = (bf16[512,384]{1,0:T(8,128)(2,1)S(1)}, bf16[512,384]{1,0:T(8,128)(2,1)}, u32[]{:S(2)}, u32[]{:S(2)}) collective-permute-start(bf16[512,384]{1,0:T(8,128)(2,1)S(1)} %get-tuple-element.119.v_ref), channel_id=1, source_target_pairs={{0,4},{1,5},{2,6},{3,7},{8,12},{9,13},{10,14},{11,15},{16,20},{17,... | collective-permute-start | bytes 1179656 | tf_op jit(solution)/shard_map/ppermute | solution.py:468
  97.5 39.8 %collective-permute-start.2 = (bf16[512,384]{1,0:T(8,128)(2,1)}, bf16[512,384]{1,0:T(8,128)(2,1)}, u32[]{:S(2)}, u32[]{:S(2)}) collective-permute-start(bf16[512,384]{1,0:T(8,128)(2,1)} %get-tuple-element.43), channel_id=1, source_target_pairs={{0,4},{1,5},{2,6},{3,7},{8,12},{9,13},{10,14},{11,15},{16,20},{17,... | collective-permute-start | bytes 1179656 | tf_op jit(solution)/shard_map/ppermute | solution.py:468
  136.0 63.0 %copy-start.1 = (bf16[128,8,4,384]{3,1,2,0:T(8,128)(2,1)}, bf16[128,8,4,384]{3,1,2,0:T(8,128)(2,1)S(1)}, u32[]{:S(2)}) copy-start(bf16[128,8,4,384]{3,1,2,0:T(8,128)(2,1)S(1)} %copy.77) | copy-start | bytes 9437188
  192.5 6.5 %copy-start.20 = (bf16[1,512,1536]{2,1,0:T(8,128)(2,1)S(1)}, bf16[1,512,1536]{2,1,0:T(8,128)(2,1)}, u32[]{:S(2)}) copy-start(bf16[1,512,1536]{2,1,0:T(8,128)(2,1)} %param.17) | copy-start | bytes 4718596
  204.6 48.3 %copy-start.6 = (bf16[48,8,4,384]{3,1,2,0:T(8,128)(2,1)S(1)}, bf16[48,8,4,384]{3,1,2,0:T(8,128)(2,1)}, u32[]{:S(2)}) copy-start(bf16[48,8,4,384]{3,1,2,0:T(8,128)(2,1)} %copy.76) | copy-start | bytes 3538948
  272.5 3.8 collective-permute-start.4
  273.8 3.8 collective-permute-start.5
  278.4 16.3 %copy-start.4 = (bf16[1,512,1536]{2,1,0:T(8,128)(2,1)S(1)}, bf16[1,512,1536]{2,1,0:T(8,128)(2,1)}, u32[]{:S(2)}) copy-start(bf16[1,512,1536]{2,1,0:T(8,128)(2,1)} %param.15) | copy-start | bytes 4718596
  278.4 16.3 %copy-start.16 = (f32[1536]{0:T(1024)S(1)}, f32[1536]{0:T(1024)}, u32[]{:S(2)}) copy-start(f32[1536]{0:T(1024)} %copy-done.15) | copy-start | bytes 18436
  278.4 16.3 %copy-start.19 = (f32[512]{0:T(512)S(1)}, f32[512]{0:T(512)}, u32[]{:S(2)}) copy-start(f32[512]{0:T(512)} %copy-done.18) | copy-start | bytes 6148
  290.1 3.3 collective-permute-start.6
  303.1 127.2 %reduce-scatter.9.cloned.1.call-start = ((), (), s32[]{:S(2)}) async-start(), calls=%async_computation.10 | async-start | bytes 7077888 | tf_op jit(solution)/shard_map/reduce_scatter | solution.py:489
  311.6 207.8 %reduce-scatter.7.cloned.1.call-start = ((), (), s32[]{:S(2)}) async-start(), calls=%async_computation.9 | async-start | bytes 1327104 | tf_op jit(solution)/shard_map/reduce_scatter | solution.py:489
  316.3 206.2 %reduce-scatter.11.cloned.1.call-start = ((), (), s32[]{:S(2)}) async-start(), calls=%async_computation.12 | async-start | bytes 3538944 | tf_op jit(solution)/shard_map/reduce_scatter | solution.py:489
  328.8 197.5 %all-gather.12.cloned.1.call-start = ((), (), s32[]{:S(2)}) async-start(), calls=%async_computation.8 | async-start | bytes 1916928 | tf_op jit(solution)/shard_map/all_gather | solution.py:490
  360.0 171.8 %all-gather.14.cloned.1.call-start = ((), (), s32[]{:S(2)}) async-start(), calls=%async_computation.11 | async-start | bytes 2359296 | tf_op jit(solution)/shard_map/all_gather | solution.py:490
  527.2 3.1 copy-start
  531.7 3.6 copy-start.5
  535.3 2.5 copy-start.2
  (10 other events, 13.1 us)
Sparse Core Ops, SparseCore 0:
  14.1 57.6 all-gather.5
  74.0 46.7 all-gather.7
  122.4 63.5 all-gather.9
  303.3 56.6 reduce-scatter.4
  362.1 68.1 reduce-scatter.8
  433.0 31.4 reduce-scatter.6
  467.4 39.3 reduce-scatter.10
  508.3 8.0 all-gather.11
  518.0 10.9 all-gather.13
